TPU v7x, 256 devices: a whole 4x4x8 slice. The times are simulated.
256 devices in a mesh: seq: 32 (over z, y_lo, core), head: 8 (over y_hi, x).
Axes of the slice: x: 4, y: 4 (y_hi: 2, y_lo: 2; y = y_hi * 2 + y_lo), z: 8, core: 2. Of those that a mesh axis runs over, the one named last changes fastest.
Arguments:
- queries: bfloat16 [32768, 4096], P('seq', 'head'), may hold values from -6 to 6
- keys: bfloat16 [32768, 4096], P('seq', 'head'), may hold values from -6 to 6
- values: bfloat16 [32768, 4096], P('seq', 'head'), may hold values from -6 to 6
- out_weight: bfloat16 [4096, 4096], P('head'), may hold values from -1.5 to 1.5
Outputs:
- mixed: bfloat16 [32768, 4096], P('seq', 'head')
All inputs are finite; a program needn't handle non-finite values.
Results may differ from a plain program's by a relative error of at most 0.015.
Values may be sent and summed in bfloat16 or wider, within the bound.
A program may use at most 192 MiB of HBM per device.

v0:
```python
import math

import jax
import jax.numpy as jnp
from jax import lax
from jax.sharding import PartitionSpec as P

HEAD_DIM = 128
SEG1 = 2048
SEG2 = 8192


NEG_FILL = -1e30


def passed_along(value, axis, steps):
    count = lax.axis_size(axis)
    leading, last = (max(0, -steps), min(count, count - steps))
    return lax.ppermute(value, axis, [(source, source + steps) for source in range(leading, last)])


def attend_block(query, key_rows, value_rows, valid, scale):
    scores = jnp.einsum("qhd,khd->hqk", query, key_rows, preferred_element_type=jnp.float32) * scale
    scores = jnp.where(valid, scores, NEG_FILL)
    peak = jnp.max(scores, axis=-1)
    weights = jnp.where(valid, jnp.exp(scores - peak[..., None]), 0.0)
    total = jnp.sum(weights, axis=-1)
    numer = jnp.einsum(
        "hqk,khd->hqd", weights.astype(jnp.bfloat16), value_rows, preferred_element_type=jnp.float32
    )
    return (numer, peak, total)


def absorb_block(state, query, key_rows, value_rows, valid, scale):
    numer, peak, total = state
    scores = jnp.einsum("qhd,khd->hqk", query, key_rows, preferred_element_type=jnp.float32) * scale
    scores = jnp.where(valid, scores, NEG_FILL)
    new_peak = jnp.maximum(peak, jnp.max(scores, axis=-1))
    weights = jnp.where(valid, jnp.exp(scores - new_peak[..., None]), 0.0)
    added = jnp.einsum(
        "hqk,khd->hqd", weights.astype(jnp.bfloat16), value_rows, preferred_element_type=jnp.float32
    )
    return (added, new_peak, jnp.sum(weights, axis=-1))


def take_dilated(source, stride, offsets):
    count = source.shape[0] // stride
    shaped = source.reshape(count, stride, offsets.shape[0], -1)
    picker = (jnp.arange(stride)[:, None] == offsets[None, :]).astype(source.dtype)
    return jnp.sum(shaped * picker[None, :, :, None], axis=1).reshape(count, -1)


def spread_rows(state, stride, offsets):
    numer, peak, total = state
    heads_here, count = peak.shape
    picker = jnp.arange(stride)[None, :] == offsets[:, None]
    numer_full = jnp.where(picker[:, None, :, None], numer[:, :, None, :], 0.0).reshape(
        heads_here, count * stride, -1
    )
    peak_full = jnp.where(picker[:, None, :], peak[:, :, None], NEG_FILL).reshape(
        heads_here, count * stride
    )
    total_full = jnp.where(picker[:, None, :], total[:, :, None], 0.0).reshape(
        heads_here, count * stride
    )
    return (numer_full, peak_full, total_full)


def shards(queries, keys, values, out_weight):
    tok_rows = queries.shape[0]
    heads_here = queries.shape[1] // HEAD_DIM
    scale = 1.0 / math.sqrt(HEAD_DIM)
    seq_index = lax.axis_index("seq")
    head_index = lax.axis_index("head")
    head_ids = head_index * heads_here + jnp.arange(heads_here)
    query_pos = seq_index * tok_rows + jnp.arange(tok_rows)
    near_span = SEG1 // tok_rows
    near_keys, near_values = (keys, values)
    level_bit = 0
    moved = passed_along((near_keys, near_values), "seq", 1 << level_bit)
    near_keys = jnp.concatenate([moved[0], near_keys], axis=0)
    near_values = jnp.concatenate([moved[1], near_values], axis=0)
    near_pos = (seq_index - near_span + 1) * tok_rows + jnp.arange(near_span * tok_rows)
    near_start = seq_index // near_span * near_span * tok_rows
    near_valid = (near_pos[None, :] <= query_pos[:, None]) & (near_pos[None, :] >= near_start)

    def near_head(head_slot):
        column = head_slot * HEAD_DIM
        query = lax.dynamic_slice_in_dim(queries, column, HEAD_DIM, 1)[:, None, :]
        key_rows = lax.dynamic_slice_in_dim(near_keys, column, HEAD_DIM, 1)[:, None, :]
        value_rows = lax.dynamic_slice_in_dim(near_values, column, HEAD_DIM, 1)[:, None, :]
        numer, peak, total = attend_block(query, key_rows, value_rows, near_valid[None], scale)
        return (numer[0], peak[0], total[0])

    near_state = lax.map(near_head, jnp.arange(heads_here))
    mid_offsets = head_ids % 4
    far_offsets = head_ids % 16
    mid_count = tok_rows // 4
    far_count = tok_rows // 16
    mid_query = take_dilated(queries, 4, mid_offsets).reshape(mid_count, heads_here, HEAD_DIM)
    far_query = take_dilated(queries, 16, far_offsets).reshape(far_count, heads_here, HEAD_DIM)
    mid_keys = take_dilated(keys, 4, mid_offsets)
    mid_values = take_dilated(values, 4, mid_offsets)
    mid_qpos = seq_index * tok_rows + mid_offsets[:, None] + 4 * jnp.arange(mid_count)[None, :]
    far_qpos = seq_index * tok_rows + far_offsets[:, None] + 16 * jnp.arange(far_count)[None, :]
    mid_span = SEG2 // tok_rows
    mid_start = seq_index // mid_span * mid_span * tok_rows
    empty_far = (
        jnp.zeros((heads_here, far_count, HEAD_DIM), jnp.float32),
        jnp.full((heads_here, far_count), NEG_FILL, jnp.float32),
        jnp.zeros((heads_here, far_count), jnp.float32),
    )
    block_keys, block_values = (mid_keys, mid_values)
    for level_bit in range(mid_span.bit_length() - 1):
        moved = passed_along((block_keys, block_values), "seq", 1 << level_bit)
        block_keys = jnp.concatenate([moved[0], block_keys], axis=0)
        block_values = jnp.concatenate([moved[1], block_values], axis=0)
    key_index = jnp.arange(mid_span * mid_count)
    mid_kpos = (
        (seq_index - mid_span + 1) * tok_rows
        + (key_index // mid_count * tok_rows + 4 * (key_index % mid_count))[None, :]
        + mid_offsets[:, None]
    )
    mid_valid = (mid_kpos[:, None, :] <= mid_qpos[:, :, None]) & (mid_kpos[:, None, :] >= mid_start)
    mid_state = attend_block(
        mid_query,
        block_keys.reshape(-1, heads_here, HEAD_DIM),
        block_values.reshape(-1, heads_here, HEAD_DIM),
        mid_valid,
        scale,
    )
    far_keys = take_dilated(keys, 16, far_offsets)
    far_values = take_dilated(values, 16, far_offsets)
    piece = (
        lax.all_gather(far_keys, "seq", axis=0, tiled=True),
        lax.all_gather(far_values, "seq", axis=0, tiled=True),
    )
    count = piece[0].shape[0]
    row_index = jnp.arange(count)
    key_pos = (row_index // far_count * tok_rows + 16 * (row_index % far_count))[
        None, :
    ] + far_offsets[:, None]
    valid = key_pos[:, None, :] <= far_qpos[:, :, None]
    far_state = absorb_block(
        empty_far,
        far_query,
        piece[0].reshape(count, heads_here, HEAD_DIM),
        piece[1].reshape(count, heads_here, HEAD_DIM),
        valid,
        scale,
    )
    levels = (
        near_state,
        spread_rows(mid_state, 4, mid_offsets),
        spread_rows(far_state, 16, far_offsets),
    )
    top = jnp.maximum(jnp.maximum(levels[0][1], levels[1][1]), levels[2][1])
    numer = jnp.zeros_like(levels[0][0])
    total = jnp.zeros_like(levels[0][2])
    for level in levels:
        factor = jnp.exp(level[1] - top)
        numer = numer + level[0] * factor[..., None]
        total = total + level[2] * factor
    attended = (
        jnp.transpose(numer / total[..., None], (1, 0, 2))
        .reshape(tok_rows, -1)
        .astype(jnp.bfloat16)
    )
    terms = jnp.dot(attended, out_weight, preferred_element_type=jnp.float32)
    return lax.psum_scatter(terms.astype(jnp.bfloat16), "head", scatter_dimension=1, tiled=True)


def solution(mesh):
    placed = (P("seq", "head"), P("seq", "head"), P("seq", "head"), P("head", None))
    return jax.shard_map(
        shards, mesh=mesh, in_specs=placed, out_specs=P("seq", "head"), check_vma=False
    )
```

profile of v0, /device:TPU:1, one launch (start us, length us, event | category | flops | bytes accessed | tf_op | source)
XLA Modules:
  0.0 336.2 jit_solution(7610765403443138857)
XLA Ops:
  10.3 4.5 %multiply_reduce_fusion = (bf16[64,4,128]{2,1,0:T(4,128)(2,1)S(1)}, bf16[64,4,128]{2,1,0:T(4,128)(2,1)S(1)}, bf16[64,4,128]{2,1,0:T(4,128)(2,1)S(1)}) fusion(bf16[64,16,4,128]{3,2,1,0:T(4,128)(2,1)} %reshape.490, bf16[16,4]{1,0:T(8,128)(2,1)S(1)} %fusion.70, bf16[64,16,4,128]{3,2,1,0:T(4,128)(2,1)} %reshape.485, bf16[64,16,4,128]{3,2,1,0:T(4,128)(2,1)S(1)} %reshape.484), kind=kLoop, calls=%fused_computation.54 | loop fusion | flops 3047424 | bytes 3342464 | tf_op jit(solution)/shard_map/reduce_sum | solution.py:50
  15.5 4.6 %collective-permute-start = (bf16[1024,512]{1,0:T(8,128)(2,1)S(1)}, bf16[1024,512]{1,0:T(8,128)(2,1)}, u32[]{:S(2)}, u32[]{:S(2)}) collective-permute-start(bf16[1024,512]{1,0:T(8,128)(2,1)S(1)} %copy-done), channel_id=1, source_target_pairs={{0,8},{8,16},{16,24},{24,32},{32,40},{40,48},{48,56},{56,64},{64,7... | collective-permute-start | bytes 3145736 | tf_op jit(solution)/shard_map/ppermute | solution.py:19
  25.7 5.3 %multiply_reduce_fusion.1 = (bf16[256,4,128]{2,1,0:T(4,128)(2,1)}, bf16[256,4,128]{2,1,0:T(4,128)(2,1)S(1)}, bf16[256,4,128]{2,1,0:T(4,128)(2,1)}) fusion(bf16[256,4,4,128]{3,2,1,0:T(4,128)(2,1)} %reshape.488, bf16[4,4]{1,0:T(4,128)(2,1)S(1)} %get-tuple-element.130, bf16[256,4,4,128]{3,2,1,0:T(4,128)(2,1)} %reshape.482, bf16[256,4,4,128]{3,2,1,0:T(4,128)(2,1)S(1)} %reshape.481), kind=kLoop, calls=%fused_computation.57 | loop fusion | flops 2752512 | bytes 3932192 | tf_op jit(solution)/shard_map/reduce_sum | solution.py:50
  31.2 3.8 %collective-permute-start.2 = (bf16[256,512]{0,1:T(8,128)(2,1)S(1)}, bf16[256,512]{0,1:T(8,128)(2,1)S(1)}, u32[]{:S(2)}, u32[]{:S(2)}) collective-permute-start(bf16[256,512]{0,1:T(8,128)(2,1)S(1)} %bitcast.57), channel_id=1, source_target_pairs={{0,8},{8,16},{16,24},{24,32},{32,40},{40,48},{48,56},{56,64},{64,7... | collective-permute-start | bytes 786440 | tf_op jit(solution)/shard_map/ppermute | solution.py:19
  39.8 10.1 %collective-permute-done.2 = bf16[256,512]{0,1:T(8,128)(2,1)S(1)} collective-permute-done((bf16[256,512]{0,1:T(8,128)(2,1)S(1)}, bf16[256,512]{0,1:T(8,128)(2,1)S(1)}, u32[]{:S(2)}, u32[]{:S(2)}) %collective-permute-start.2) | collective-permute-done | bytes 262176 | tf_op jit(solution)/shard_map/ppermute | solution.py:19
  50.7 4.8 %collective-permute-start.3 = (bf16[512,512]{0,1:T(8,128)(2,1)}, bf16[512,512]{0,1:T(8,128)(2,1)}, u32[]{:S(2)}, u32[]{:S(2)}) collective-permute-start(bf16[512,512]{0,1:T(8,128)(2,1)} %pad_maximum_fusion.4), channel_id=1, source_target_pairs={{0,16},{8,24},{16,32},{24,40},{32,48},{40,56},{48,64},{56,72},{64,... | collective-permute-start | bytes 1572872 | tf_op jit(solution)/shard_map/ppermute | solution.py:19
  65.3 3.7 %collective-permute-done.3 = bf16[512,512]{0,1:T(8,128)(2,1)} collective-permute-done((bf16[512,512]{0,1:T(8,128)(2,1)}, bf16[512,512]{0,1:T(8,128)(2,1)}, u32[]{:S(2)}, u32[]{:S(2)}) %collective-permute-start.3) | collective-permute-done | bytes 524320 | tf_op jit(solution)/shard_map/ppermute | solution.py:19
  71.1 11.2 %collective-permute-done.6 = bf16[512,512]{0,1:T(8,128)(2,1)} collective-permute-done((bf16[512,512]{0,1:T(8,128)(2,1)}, bf16[512,512]{0,1:T(8,128)(2,1)}, u32[]{:S(2)}, u32[]{:S(2)}) %collective-permute-start.6) | collective-permute-done | bytes 524320 | tf_op jit(solution)/shard_map/ppermute | solution.py:19
  86.6 2.7 collective-permute-start.7
  94.1 2.7 pad_maximum_fusion
  96.8 2.7 pad_maximum_fusion.1
  99.5 54.4 %while.16 = (s32[]{:T(128)}, f32[4,1024,128]{2,1,0:T(8,128)}, f32[4,1024]{1,0:T(4,128)S(1)}, f32[4,1024]{1,0:T(4,128)S(1)}, s32[4]{0:T(128)S(1)}, /*index=5*/bf1...) while((s32[]{:T(128)}, f32[4,1024,128]{2,1,0:T(8,128)}, ...), condition=%wide.region_3.4_spmd.clone.clone, body=%wide.region_0.3_spmd.clone.sunk.clone | while | flops 1113585664 | bytes 27077832 | solution.py:95
  101.0 3.5 %fusion.95 = (f32[1024]{0:T(1024)S(1)}, f32[1024,2048]{1,0:T(8,128)S(1)}) fusion(s32[2048]{0:T(1024)S(1)} %get-tuple-element.272, s32[1024]{0:T(1024)S(1)} %get-tuple-element.271, pred[2048]{0:T(1024)(128)(4,1)S(1)} %get-tuple-element.273, bf16[2048,512]{1,0:T(8,128)(2,1)} %get-tuple-element.269, s32[]{:T(128)S(6)} %select_n.271, ...), kind=kOutput, calls=%fused_computation.4.clone.1.clone | convolution fusion | flops 547355648 | bytes 9194496 | tf_op jit(solution)/shard_map/while/body/eval_jaxpr/qhd,khd->hqk/dot_general | solution.py:23
  104.5 3.7 %fusion.97 = f32[1024]{0:T(1024)S(1)} fusion(f32[1024]{0:T(1024)S(1)} %get-tuple-element.222, f32[1024,2048]{1,0:T(8,128)S(1)} %get-tuple-element.221, pred[2048]{0:T(1024)(128)(4,1)S(1)} %get-tuple-element.273, s32[1024]{0:T(1024)S(1)} %get-tuple-element.271, s32[2048]{0:T(1024)S(1)} %get-tuple-element.272), kind=kLoop, calls=%fused_computation.15.clone.1.clone | loop fusion | flops 14679040 | bytes 8411136 | tf_op jit(solution)/shard_map/while/body/eval_jaxpr/reduce_sum | solution.py:27
  108.2 5.0 %fusion.96 = f32[4,1024,128]{2,1,0:T(8,128)} fusion(f32[4,1024,128]{2,1,0:T(8,128)} %get-tuple-element.252, s32[]{:T(128)S(6)} %copy.70, bf16[2048,512]{1,0:T(8,128)(2,1)} %get-tuple-element.270, s32[]{:T(128)S(6)} %select_n.271, f32[1024,2048]{1,0:T(8,128)S(1)} %get-tuple-element.221, s32[2048]{0:T(1024)S(1)} %get-tuple-element.272, ...), kind=kOutput, calls=%fused_computation.8.clone.1.clone | convolution fusion | flops 551550976 | bytes 9455624 | tf_op jit(solution)/shard_map/while/body/eval_jaxpr/hqk,khd->hqd/dot_general | solution.py:28
  114.5 3.6 %fusion.95 = (f32[1024]{0:T(1024)S(1)}, f32[1024,2048]{1,0:T(8,128)S(1)}) fusion(s32[2048]{0:T(1024)S(1)} %get-tuple-element.272, s32[1024]{0:T(1024)S(1)} %get-tuple-element.271, pred[2048]{0:T(1024)(128)(4,1)S(1)} %get-tuple-element.273, bf16[2048,512]{1,0:T(8,128)(2,1)} %get-tuple-element.269, s32[]{:T(128)S(6)} %select_n.271, ...), kind=kOutput, calls=%fused_computation.4.clone.1.clone | convolution fusion | flops 547355648 | bytes 9194496 | tf_op jit(solution)/shard_map/while/body/eval_jaxpr/qhd,khd->hqk/dot_general | solution.py:23
  118.1 3.7 %fusion.97 = f32[1024]{0:T(1024)S(1)} fusion(f32[1024]{0:T(1024)S(1)} %get-tuple-element.222, f32[1024,2048]{1,0:T(8,128)S(1)} %get-tuple-element.221, pred[2048]{0:T(1024)(128)(4,1)S(1)} %get-tuple-element.273, s32[1024]{0:T(1024)S(1)} %get-tuple-element.271, s32[2048]{0:T(1024)S(1)} %get-tuple-element.272), kind=kLoop, calls=%fused_computation.15.clone.1.clone | loop fusion | flops 14679040 | bytes 8411136 | tf_op jit(solution)/shard_map/while/body/eval_jaxpr/reduce_sum | solution.py:27
  121.8 4.9 %fusion.96 = f32[4,1024,128]{2,1,0:T(8,128)} fusion(f32[4,1024,128]{2,1,0:T(8,128)} %get-tuple-element.252, s32[]{:T(128)S(6)} %copy.70, bf16[2048,512]{1,0:T(8,128)(2,1)} %get-tuple-element.270, s32[]{:T(128)S(6)} %select_n.271, f32[1024,2048]{1,0:T(8,128)S(1)} %get-tuple-element.221, s32[2048]{0:T(1024)S(1)} %get-tuple-element.272, ...), kind=kOutput, calls=%fused_computation.8.clone.1.clone | convolution fusion | flops 551550976 | bytes 9455624 | tf_op jit(solution)/shard_map/while/body/eval_jaxpr/hqk,khd->hqd/dot_general | solution.py:28
  128.1 3.6 %fusion.95 = (f32[1024]{0:T(1024)S(1)}, f32[1024,2048]{1,0:T(8,128)S(1)}) fusion(s32[2048]{0:T(1024)S(1)} %get-tuple-element.272, s32[1024]{0:T(1024)S(1)} %get-tuple-element.271, pred[2048]{0:T(1024)(128)(4,1)S(1)} %get-tuple-element.273, bf16[2048,512]{1,0:T(8,128)(2,1)} %get-tuple-element.269, s32[]{:T(128)S(6)} %select_n.271, ...), kind=kOutput, calls=%fused_computation.4.clone.1.clone | convolution fusion | flops 547355648 | bytes 9194496 | tf_op jit(solution)/shard_map/while/body/eval_jaxpr/qhd,khd->hqk/dot_general | solution.py:23
  131.7 3.7 %fusion.97 = f32[1024]{0:T(1024)S(1)} fusion(f32[1024]{0:T(1024)S(1)} %get-tuple-element.222, f32[1024,2048]{1,0:T(8,128)S(1)} %get-tuple-element.221, pred[2048]{0:T(1024)(128)(4,1)S(1)} %get-tuple-element.273, s32[1024]{0:T(1024)S(1)} %get-tuple-element.271, s32[2048]{0:T(1024)S(1)} %get-tuple-element.272), kind=kLoop, calls=%fused_computation.15.clone.1.clone | loop fusion | flops 14679040 | bytes 8411136 | tf_op jit(solution)/shard_map/while/body/eval_jaxpr/reduce_sum | solution.py:27
  135.3 4.9 %fusion.96 = f32[4,1024,128]{2,1,0:T(8,128)} fusion(f32[4,1024,128]{2,1,0:T(8,128)} %get-tuple-element.252, s32[]{:T(128)S(6)} %copy.70, bf16[2048,512]{1,0:T(8,128)(2,1)} %get-tuple-element.270, s32[]{:T(128)S(6)} %select_n.271, f32[1024,2048]{1,0:T(8,128)S(1)} %get-tuple-element.221, s32[2048]{0:T(1024)S(1)} %get-tuple-element.272, ...), kind=kOutput, calls=%fused_computation.8.clone.1.clone | convolution fusion | flops 551550976 | bytes 9455624 | tf_op jit(solution)/shard_map/while/body/eval_jaxpr/hqk,khd->hqd/dot_general | solution.py:28
  141.7 3.5 %fusion.95 = (f32[1024]{0:T(1024)S(1)}, f32[1024,2048]{1,0:T(8,128)S(1)}) fusion(s32[2048]{0:T(1024)S(1)} %get-tuple-element.272, s32[1024]{0:T(1024)S(1)} %get-tuple-element.271, pred[2048]{0:T(1024)(128)(4,1)S(1)} %get-tuple-element.273, bf16[2048,512]{1,0:T(8,128)(2,1)} %get-tuple-element.269, s32[]{:T(128)S(6)} %select_n.271, ...), kind=kOutput, calls=%fused_computation.4.clone.1.clone | convolution fusion | flops 547355648 | bytes 9194496 | tf_op jit(solution)/shard_map/while/body/eval_jaxpr/qhd,khd->hqk/dot_general | solution.py:23
  145.2 3.7 %fusion.97 = f32[1024]{0:T(1024)S(1)} fusion(f32[1024]{0:T(1024)S(1)} %get-tuple-element.222, f32[1024,2048]{1,0:T(8,128)S(1)} %get-tuple-element.221, pred[2048]{0:T(1024)(128)(4,1)S(1)} %get-tuple-element.273, s32[1024]{0:T(1024)S(1)} %get-tuple-element.271, s32[2048]{0:T(1024)S(1)} %get-tuple-element.272), kind=kLoop, calls=%fused_computation.15.clone.1.clone | loop fusion | flops 14679040 | bytes 8411136 | tf_op jit(solution)/shard_map/while/body/eval_jaxpr/reduce_sum | solution.py:27
  148.9 5.0 %fusion.96 = f32[4,1024,128]{2,1,0:T(8,128)} fusion(f32[4,1024,128]{2,1,0:T(8,128)} %get-tuple-element.252, s32[]{:T(128)S(6)} %copy.70, bf16[2048,512]{1,0:T(8,128)(2,1)} %get-tuple-element.270, s32[]{:T(128)S(6)} %select_n.271, f32[1024,2048]{1,0:T(8,128)S(1)} %get-tuple-element.221, s32[2048]{0:T(1024)S(1)} %get-tuple-element.272, ...), kind=kOutput, calls=%fused_computation.8.clone.1.clone | convolution fusion | flops 551550976 | bytes 9455624 | tf_op jit(solution)/shard_map/while/body/eval_jaxpr/hqk,khd->hqd/dot_general | solution.py:28
  157.0 5.5 %fusion.18 = (f32[4,256]{1,0:T(4,128)S(1)}, f32[4,256,2048]{2,1,0:T(8,128)}) fusion(s32[4,256]{1,0:T(4,128)S(1)} %broadcast_add_fusion.2, s32[4,2048]{1,0:T(4,128)S(1)} %broadcast_add_fusion.1, pred[4,2048]{1,0:T(4,128)(4,1)S(1)} %broadcast_compare_fusion, bf16[256,4,128]{2,0,1:T(8,128)(2,1)S(1)} %copy-done.8, bf16[256,4,128]{2,0,1:T(8,128)(2,1)} %copy.33, ...), kind=kOutput, calls=%fused_computation.20 | convolution fusion | flops 555744256 | bytes 10797056 | tf_op jit(solution)/shard_map/qhd,khd->hqk/dot_general | solution.py:23
  163.1 5.7 %fusion.21 = f32[4,256]{1,0:T(4,128)S(1)} fusion(f32[4,256]{1,0:T(4,128)S(1)} %get-tuple-element.131, f32[4,256,2048]{2,1,0:T(8,128)} %get-tuple-element.132, pred[4,2048]{1,0:T(4,128)(4,1)S(1)} %broadcast_compare_fusion, s32[4,256]{1,0:T(4,128)S(1)} %broadcast_add_fusion.2, s32[4,2048]{1,0:T(4,128)S(1)} %broadcast_add_fusion.1), kind=kLoop, calls=%fused_computation.23 | loop fusion | flops 14679040 | bytes 8441856 | tf_op jit(solution)/shard_map/reduce_sum | solution.py:27
  169.2 5.4 %fusion.19 = f32[4,256,128]{2,1,0:T(8,128)S(1)} fusion(f32[4,256,2048]{2,1,0:T(8,128)} %get-tuple-element.132, f32[4,256]{1,0:T(4,128)S(1)} %get-tuple-element.131, s32[4,256]{1,0:T(4,128)S(1)} %broadcast_add_fusion.2, s32[4,2048]{1,0:T(4,128)S(1)} %broadcast_add_fusion.1, pred[4,2048]{1,0:T(4,128)(4,1)S(1)} %broadcast_compare_fusion, ...), kind=kOutput, calls=%fused_computation.21 | convolution fusion | flops 559939584 | bytes 11059200 | tf_op jit(solution)/shard_map/hqk,khd->hqd/dot_general | solution.py:28
  174.7 4.0 %copy.36 = bf16[2048,512]{0,1:T(8,128)(2,1)} copy(bf16[2048,512]{1,0:T(8,128)(2,1)} %all-gather.3.cloned.1.call-done) | data formatting | bytes 4194304 | tf_op jit(solution)/shard_map/all_gather | solution.py:135
  181.6 4.0 %copy.44 = bf16[2048,512]{0,1:T(8,128)(2,1)} copy(bf16[2048,512]{1,0:T(8,128)(2,1)} %all-gather.5.cloned.1.call-done) | data formatting | bytes 4194304 | tf_op jit(solution)/shard_map/all_gather | solution.py:136
  188.9 6.3 %fusion.41 = bf16[4,1024,128]{2,1,0:T(8,128)(2,1)S(1)} fusion(f32[4,1024,128]{2,1,0:T(8,128)S(1)} %bitcast.54, f32[4,1024,128]{2,1,0:T(8,128)} %get-tuple-element.54, f32[4,1024]{1,0:T(4,128)S(1)} %get-tuple-element.123, f32[4,1024]{1,0:T(4,128)S(1)} %get-tuple-element.126, f32[4,64,128]{2,1,0:T(8,128)S(1)} %fusion.44, f32[4,1024]{1,0:T(4,128)S(1)} %get-tuple-element.125, ...), kind=kLoop, calls=%fused_computation.48 | loop fusion | flops 4718592 | bytes 5447680 | tf_op jit(solution)/shard_map/convert_element_type | solution.py:167
  195.7 8.9 %convolution_convert_fusion = bf16[1024,4096]{1,0:T(8,128)(2,1)} fusion(bf16[1024,512]{0,1:T(8,128)(2,1)S(1)} %bitcast.66, bf16[512,4096]{1,0:T(8,128)(2,1)} %param.9), kind=kOutput, calls=%fused_computation.19 | convolution fusion | flops 4299161600 | bytes 13631488 | tf_op jit(solution)/shard_map/dot_general | solution.py:169
  204.7 125.0 %reduce-scatter.2.cloned.1.call-done = bf16[1024,512]{1,0:T(8,128)(2,1)} async-done(((bf16[1024,4096]{1,0:T(8,128)(2,1)}), bf16[1024,512]{1,0:T(8,128)(2,1)}) %reduce-scatter.2.cloned.1.call-update) | async-done | bytes 1048592 | tf_op jit(solution)/shard_map/reduce_scatter | solution.py:170
  (118 shorter events, 50.3 us)
Async XLA Ops:
  6.5 1.5 copy-start
  6.5 168.2 %all-gather.3.cloned.1.call-start = ((), (), s32[]{:S(2)}) async-start(), calls=%async_computation.1 | async-start | bytes 2162688 | tf_op jit(solution)/shard_map/all_gather | solution.py:135
  6.6 32.3 %copy-start.11 = (s32[4]{0:T(128)}, s32[4]{0:T(128)S(1)}, u32[]{:S(2)}) copy-start(s32[4]{0:T(128)S(1)} %get-tuple-element.135) | copy-start | bytes 52
  6.6 2.6 copy-start.1
  15.4 166.1 %all-gather.5.cloned.1.call-start = ((), (), s32[]{:S(2)}) async-start(), calls=%async_computation.2 | async-start | bytes 2162688 | tf_op jit(solution)/shard_map/all_gather | solution.py:136
  15.5 78.6 %collective-permute-start = (bf16[1024,512]{1,0:T(8,128)(2,1)S(1)}, bf16[1024,512]{1,0:T(8,128)(2,1)}, u32[]{:S(2)}, u32[]{:S(2)}) collective-permute-start(bf16[1024,512]{1,0:T(8,128)(2,1)S(1)} %copy-done), channel_id=1, source_target_pairs={{0,8},{8,16},{16,24},{24,32},{32,40},{40,48},{48,56},{56,64},{64,7... | collective-permute-start | bytes 3145736 | tf_op jit(solution)/shard_map/ppermute | solution.py:19
  20.1 76.7 %collective-permute-start.1 = (bf16[1024,512]{1,0:T(8,128)(2,1)S(1)}, bf16[1024,512]{1,0:T(8,128)(2,1)}, u32[]{:S(2)}, u32[]{:S(2)}) collective-permute-start(bf16[1024,512]{1,0:T(8,128)(2,1)S(1)} %copy-done.1), channel_id=1, source_target_pairs={{0,8},{8,16},{16,24},{24,32},{32,40},{40,48},{48,56},{56,64},{64,7... | collective-permute-start | bytes 3145736 | tf_op jit(solution)/shard_map/ppermute | solution.py:19
  31.0 28.9 %copy-start.2 = (bf16[256,4,128]{2,1,0:T(4,128)(2,1)S(1)}, bf16[256,4,128]{2,1,0:T(4,128)(2,1)}, u32[]{:S(2)}) copy-start(bf16[256,4,128]{2,1,0:T(4,128)(2,1)} %get-tuple-element.98) | copy-start | bytes 786436
  31.2 18.7 %collective-permute-start.2 = (bf16[256,512]{0,1:T(8,128)(2,1)S(1)}, bf16[256,512]{0,1:T(8,128)(2,1)S(1)}, u32[]{:S(2)}, u32[]{:S(2)}) collective-permute-start(bf16[256,512]{0,1:T(8,128)(2,1)S(1)} %bitcast.57), channel_id=1, source_target_pairs={{0,8},{8,16},{16,24},{24,32},{32,40},{40,48},{48,56},{56,64},{64,7... | collective-permute-start | bytes 786440 | tf_op jit(solution)/shard_map/ppermute | solution.py:19
  36.1 19.4 %collective-permute-start.5 = (bf16[256,512]{0,1:T(8,128)(2,1)S(1)}, bf16[256,512]{0,1:T(8,128)(2,1)}, u32[]{:S(2)}, u32[]{:S(2)}) collective-permute-start(bf16[256,512]{0,1:T(8,128)(2,1)S(1)} %bitcast.61), channel_id=1, source_target_pairs={{0,8},{8,16},{16,24},{24,32},{32,40},{40,48},{48,56},{56,64},{64,7... | collective-permute-start | bytes 786440 | tf_op jit(solution)/shard_map/ppermute | solution.py:19
  38.7 291.0 %reduce-scatter.2.cloned.1.call-start = ((), (), s32[]{:S(2)}) async-start(), calls=%async_computation.3 | async-start | bytes 9437184 | tf_op jit(solution)/shard_map/reduce_scatter | solution.py:170
  39.6 22.9 %copy-start.12 = (s32[4]{0:T(128)S(1)}, s32[4]{0:T(128)}, u32[]{:S(2)}) copy-start(s32[4]{0:T(128)} %copy-done.11) | copy-start | bytes 52
  50.7 18.3 %collective-permute-start.3 = (bf16[512,512]{0,1:T(8,128)(2,1)}, bf16[512,512]{0,1:T(8,128)(2,1)}, u32[]{:S(2)}, u32[]{:S(2)}) collective-permute-start(bf16[512,512]{0,1:T(8,128)(2,1)} %pad_maximum_fusion.4), channel_id=1, source_target_pairs={{0,16},{8,24},{16,32},{24,40},{32,48},{40,56},{48,64},{56,72},{64,... | collective-permute-start | bytes 1572872 | tf_op jit(solution)/shard_map/ppermute | solution.py:19
  57.4 25.0 %collective-permute-start.6 = (bf16[512,512]{0,1:T(8,128)(2,1)}, bf16[512,512]{0,1:T(8,128)(2,1)}, u32[]{:S(2)}, u32[]{:S(2)}) collective-permute-start(bf16[512,512]{0,1:T(8,128)(2,1)} %pad_maximum_fusion.5), channel_id=1, source_target_pairs={{0,16},{8,24},{16,32},{24,40},{32,48},{40,56},{48,64},{56,72},{64,... | collective-permute-start | bytes 1572872 | tf_op jit(solution)/shard_map/ppermute | solution.py:19
  86.6 67.3 %collective-permute-start.7 = (bf16[1024,512]{0,1:T(8,128)(2,1)}, bf16[1024,512]{0,1:T(8,128)(2,1)}, u32[]{:S(2)}, u32[]{:S(2)}) collective-permute-start(bf16[1024,512]{0,1:T(8,128)(2,1)} %pad_maximum_fusion.3), channel_id=1, source_target_pairs={{0,32},{8,40},{16,48},{24,56},{32,64},{40,72},{48,80},{56,88},{64,... | collective-permute-start | bytes 3145736 | tf_op jit(solution)/shard_map/ppermute | solution.py:19
  91.5 64.2 %collective-permute-start.4 = (bf16[1024,512]{0,1:T(8,128)(2,1)}, bf16[1024,512]{0,1:T(8,128)(2,1)S(1)}, u32[]{:S(2)}, u32[]{:S(2)}) collective-permute-start(bf16[1024,512]{0,1:T(8,128)(2,1)} %pad_maximum_fusion.2), channel_id=1, source_target_pairs={{0,32},{8,40},{16,48},{24,56},{32,64},{40,72},{48,80},{56,88},{64,... | collective-permute-start | bytes 3145736 | tf_op jit(solution)/shard_map/ppermute | solution.py:19
  96.8 2.7 copy-start.9
  96.8 2.7 copy-start.10
  154.0 3.1 copy-start.4
  154.0 3.0 copy-start.5
  154.0 3.0 copy-start.8
  163.0 6.2 %copy-start.3 = (bf16[512,4,128]{2,0,1:T(8,128)(2,1)S(1)}, bf16[512,4,128]{2,0,1:T(8,128)(2,1)}, u32[]{:S(2)}) copy-start(bf16[512,4,128]{2,0,1:T(8,128)(2,1)} %copy.41) | copy-start | bytes 1572868
  163.0 6.2 %copy-start.6 = (bf16[256,4,128]{2,0,1:T(8,128)(2,1)S(1)}, bf16[256,4,128]{2,0,1:T(8,128)(2,1)}, u32[]{:S(2)}) copy-start(bf16[256,4,128]{2,0,1:T(8,128)(2,1)} %copy.43) | copy-start | bytes 786436
  163.1 6.2 %copy-start.7 = (bf16[256,4,128]{2,0,1:T(8,128)(2,1)S(1)}, bf16[256,4,128]{2,0,1:T(8,128)(2,1)}, u32[]{:S(2)}) copy-start(bf16[256,4,128]{2,0,1:T(8,128)(2,1)} %copy.42) | copy-start | bytes 786436
Sparse Core Ops, SparseCore 0:
  15.6 69.7 all-gather.2
  87.2 68.0 all-gather.4
  204.8 124.8 reduce-scatter.1
where the time goes:
time: 338 us; the launch traced here: 336 us
  waiting for transfers between devices  150 us (44%)
  matrix products  58.6 us (17%)
  other arithmetic  50.6 us (15%)
  local copies, waits for them, and re-layouts  35.6 us (11%)
  starting transfers between devices  25 us (7%)
  between operations  13.5 us (4%)
    reduce_scatter x1, waiting for transfers between devices, shards(): lax.psum_scatter(terms.astype(jnp.bfloat16), 'head', scatter_dimension=1,...  125 us
    dot_general x5, matrix products, attend_block(): jnp.einsum('hqk,khd->hqd', weights.astype(jnp.bfloat16), value_rows, pref...  25.2 us
    ppermute x8, waiting for transfers between devices, passed_along(): lax.ppermute(value, axis, [(source, source + steps) for source in range(l...  25.1 us
    ppermute x8, starting transfers between devices, passed_along(): lax.ppermute(value, axis, [(source, source + steps) for source in range(l...  24.9 us
    reduce_sum x5, other arithmetic, attend_block(): total = jnp.sum(weights, axis=-1)  20.3 us
    dot_general x5, matrix products, attend_block(): jnp.einsum('qhd,khd->hqk', query, key_rows, preferred_element_type=jnp.fl...  19.7 us
    reduce_sum x2, other arithmetic, take_dilated(): return jnp.sum(shaped * picker[None, :, :, None], axis=1).reshape(count, -1)  9.8 us
    dot_general x1, matrix products, shards(): terms = jnp.dot(attended, out_weight, preferred_element_type=jnp.float32)  8.95 us
  transfers between devices with their start and end apart: 11, of which 4 were waited for; matrix products, arithmetic and copies ran while one was open for 34% of the time, Pallas kernels for 0%

commit v1 on v0

v1 whole, which is shorter than its diff:
```python
import functools
import math

import jax
import jax.numpy as jnp
from jax import lax
from jax.experimental import pallas as pl
from jax.experimental.pallas import tpu as pltpu
from jax.sharding import PartitionSpec as P

DH = 128
ROWS = 1024
HEADS = 4
TILE = 256
NEG = -1e30
SCALE2 = math.log2(math.e) / math.sqrt(DH)
MESH = pl.DeviceIdType.MESH
bf16 = jnp.bfloat16
f32 = jnp.float32


def nt_dot(a, b):
    return lax.dot_general(a, b, (((1,), (1,)), ((), ())), preferred_element_type=f32)


def softmax_pieces(query, pieces):
    scores = []
    for key_rows, _, limit in pieces:
        score = nt_dot(query, key_rows)
        if limit is not None:
            row = lax.broadcasted_iota(jnp.int32, score.shape, 0)
            col = lax.broadcasted_iota(jnp.int32, score.shape, 1)
            score = jnp.where(col - row <= limit, score, NEG)
        scores.append(score)
    peak = functools.reduce(jnp.maximum, [jnp.max(s, axis=1, keepdims=True) for s in scores])
    both = None
    for score, (_, value_rows, _) in zip(scores, pieces):
        weights = jnp.exp2((score - peak) * SCALE2).astype(bf16)
        ones = jnp.ones(value_rows.shape, bf16)
        term = jnp.dot(weights, jnp.concatenate([value_rows, ones], axis=1), preferred_element_type=f32)
        both = term if both is None else both + term
    numer, total = both[:, :DH], both[:, DH:]
    return numer, jnp.broadcast_to(peak, numer.shape), total


def merge(one, two):
    numer1, peak1, total1 = one
    numer2, peak2, total2 = two
    top = jnp.maximum(peak1, peak2)
    f1 = jnp.exp2((peak1 - top) * SCALE2)
    f2 = jnp.exp2((peak2 - top) * SCALE2)
    return numer1 * f1 + numer2 * f2, top, total1 * f1 + total2 * f2


def attend_kernel(
    planes,
    q_hbm, k_hbm, v_hbm, w_hbm, att_ref, wg_ref,
    QA, KV, SM, SF, FQ, FKV, ACC, PK, TT, TMP, RO, RST, OB, ST,
    loc, locw, w_ss, w_rs, wf_ss, wf_rs, n_ss, n_rs, p_ss, p_rs, pv_ss, pv_rs,
    f_ss, f_rs, b_ss, b_rs, r_ss, r_rs,
):
    seq = lax.axis_index("seq")
    head = lax.axis_index("head")
    z = seq // 4
    i = seq % 4
    core = seq % 2
    zpar = z % 2
    x = head % 4
    y = head // 4

    def dev(plane, slot):
        return (plane * 4 + slot, head)

    def plane_peer(d):
        return (i + d) % 4

    pair = z + 1 - 2 * zpar
    znext = (z + 1) % planes
    zprev = (z + planes - 1) % planes
    zother = (z + planes - 1 + 2 * zpar) % planes

    loads = []
    for h in range(HEADS):
        cols = slice(h * DH, (h + 1) * DH)
        loads.append([
            pltpu.make_async_copy(q_hbm.at[:, cols], QA.at[h], loc.at[h, 0]),
            pltpu.make_async_copy(k_hbm.at[:, cols], KV.at[h, 0, pl.ds(ROWS, ROWS)], loc.at[h, 1]),
            pltpu.make_async_copy(v_hbm.at[:, cols], KV.at[h, 1, pl.ds(ROWS, ROWS)], loc.at[h, 2]),
        ])
        for copy in loads[-1]:
            copy.start()

    barrier = pltpu.get_barrier_semaphore()
    greet = [dev(z, plane_peer(d)) for d in (1, 2, 3)]
    greet += [dev(pair, s) for s in range(4)]
    greet += [dev(zother, i)]
    greet += [(seq, y * 4 + (x + d) % 4) for d in (1, 2, 3)]
    for target in greet:
        pl.semaphore_signal(barrier, inc=1, device_id=target, device_id_type=MESH)
    pl.semaphore_wait(barrier, len(greet))

    def near_copy(h, a):
        src = (k_hbm, v_hbm)[a].at[:, h * DH:(h + 1) * DH]
        return pltpu.make_async_remote_copy(
            src, KV.at[h, a, pl.ds(0, ROWS)], n_ss.at[h, a], n_rs.at[h, a],
            device_id=dev(z, i + 1 - 2 * core), device_id_type=MESH)

    @pl.when(core == 0)
    def _():
        for h in range(HEADS):
            for a in range(2):
                near_copy(h, a).start()

    half = pl.multiple_of(core * 256, 256)

    def w_copy(d, yr):
        xd = (x + d) % 4
        yd = (y + yr) % 2
        col = pl.multiple_of((yd * 4 + xd) * 512, 512)
        return pltpu.make_async_remote_copy(
            w_hbm.at[pl.ds(half, 256), pl.ds(col, 512)],
            wg_ref.at[yr, x, pl.ds(half, 256)],
            w_ss.at[d - 1, yr], w_rs.at[d - 1, yr],
            device_id=(seq, y * 4 + xd), device_id_type=MESH)

    def w_arrived(d, yr):
        xs = (x + 4 - d) % 4
        return pltpu.make_async_remote_copy(
            wg_ref.at[yr, xs, pl.ds(half, 256)],
            wg_ref.at[yr, xs, pl.ds(half, 256)],
            w_ss.at[d - 1, yr], w_rs.at[d - 1, yr],
            device_id=(seq, y * 4 + xs), device_id_type=MESH)

    def w_forward(d, yr):
        xs = (x + 4 - d) % 4
        return pltpu.make_async_remote_copy(
            wg_ref.at[yr, xs, pl.ds(half, 256)],
            wg_ref.at[yr, xs, pl.ds(half, 256)],
            wf_ss.at[d - 1, yr], wf_rs.at[d - 1, yr],
            device_id=dev(z, i + 1 - 2 * core), device_id_type=MESH)

    def w_forwarded(d, yr):
        xs = (x + 4 - d) % 4
        other = pl.multiple_of(256 - half, 256)
        return pltpu.make_async_remote_copy(
            wg_ref.at[yr, xs, pl.ds(other, 256)],
            wg_ref.at[yr, xs, pl.ds(other, 256)],
            wf_ss.at[d - 1, yr], wf_rs.at[d - 1, yr],
            device_id=dev(z, i + 1 - 2 * core), device_id_type=MESH)

    for d in (1, 3, 2):
        for yr in range(2):
            w_copy(d, yr).start()

    def w_own(yr):
        col = pl.multiple_of((((y + yr) % 2) * 4 + x) * 512, 512)
        return pltpu.make_async_copy(w_hbm.at[:, pl.ds(col, 512)], wg_ref.at[yr, x], locw.at[yr])

    for yr in range(2):
        w_own(yr).start()

    for h in range(HEADS):
        for a in range(3):
            loads[h][a].wait()
            source = QA[h] if a == 0 else KV[h, a - 1, ROWS:, :]
            TMP[a] = source.astype(f32)
            SM[h, a] = TMP[a, pl.ds(h, 256, stride=4), :].astype(bf16)
            SF[h, a] = TMP[a, pl.ds(4 * x + h, 64, stride=16), :].astype(bf16)

    def plane_copy(d, kind):
        s = plane_peer(d)
        return plane_descriptor(d, kind, s, i, s)

    def plane_arrived(d, kind):
        s = (i + 4 - d) % 4
        return plane_descriptor(d, kind, s, s, i)

    def plane_descriptor(d, kind, target, sender, slot):
        mid = pl.multiple_of(sender * 256, 256)
        far = pl.multiple_of(sender * 64, 64)
        src, dst = (
            (SF.at[slot, pl.ds(1, 2)], FKV.at[z, :, pl.ds(far, 64)]),
            (SF.at[slot, 0], FQ.at[pl.ds(far, 64)]),
            (SM.at[slot, pl.ds(1, 2)], KV.at[4, :, pl.ds(ROWS + mid, 256)]),
            (SM.at[slot, 0], QA.at[4, pl.ds(mid, 256)]),
        )[kind]
        return pltpu.make_async_remote_copy(
            src, dst, p_ss.at[d - 1, kind], p_rs.at[d - 1, kind],
            device_id=dev(z, target), device_id_type=MESH)

    def prev_copy(s):
        return pltpu.make_async_remote_copy(
            SM.at[s, pl.ds(1, 2)], KV.at[4, :, pl.ds(pl.multiple_of(i * 256, 256), 256)],
            pv_ss.at[s], pv_rs.at[i], device_id=dev(pair, s), device_id_type=MESH)

    def prev_arrived(s):
        return pltpu.make_async_remote_copy(
            SM.at[s, pl.ds(1, 2)], KV.at[4, :, pl.ds(s * 256, 256)],
            pv_ss.at[s], pv_rs.at[s], device_id=dev(pair, s), device_id_type=MESH)

    for kind in (0, 1):
        for d in (2, 3, 1):
            plane_copy(d, kind).start()

    @pl.when(zpar == 0)
    def _():
        for s in range(4):
            prev_copy(s).start()

    for kind in (2, 3):
        for d in (2, 3, 1):
            plane_copy(d, kind).start()

    own_mid = pl.multiple_of(i * 256, 256)
    own_far = pl.multiple_of(i * 64, 64)
    QA[4, pl.ds(own_mid, 256), :] = SM[i, 0]
    FQ[pl.ds(own_far, 64), :] = SF[i, 0]
    for a in range(2):
        KV[4, a, pl.ds(ROWS + own_mid, 256), :] = SM[i, 1 + a]
        FKV[z, a, pl.ds(own_far, 64), :] = SF[i, 1 + a]

    def forward(hop, slot):
        return pltpu.make_async_remote_copy(
            FKV.at[slot], FKV.at[slot], f_ss.at[hop], f_rs.at[hop],
            device_id=dev(znext, i), device_id_type=MESH)

    def backward(hop, slot):
        return pltpu.make_async_remote_copy(
            FKV.at[slot], FKV.at[slot], b_ss.at[hop], b_rs.at[hop],
            device_id=dev(zprev, i), device_id_type=MESH)

    def tiles(h, with_prev):
        for b in range(ROWS // TILE):
            rows = slice(b * TILE, (b + 1) * TILE)
            pieces = []
            if with_prev:
                pieces.append((KV[h, 0, :ROWS, :], KV[h, 1, :ROWS, :], None))
            if b:
                pieces.append((KV[h, 0, ROWS:ROWS + b * TILE, :], KV[h, 1, ROWS:ROWS + b * TILE, :], None))
            diag = slice(ROWS + b * TILE, ROWS + (b + 1) * TILE)
            pieces.append((KV[h, 0, diag, :], KV[h, 1, diag, :], 0))
            numer, peak, total = softmax_pieces(QA[h, rows, :], pieces)
            ACC[h, rows, :] = numer
            PK[h, rows, :] = peak
            TT[h, rows, :] = total

    nfwd = planes // 2
    nbwd = planes - 1 - nfwd

    def level_step(h, carry):
        @pl.when((h < 4) & (core == 1))
        def _():
            for a in range(2):
                pltpu.make_async_remote_copy(
                    KV.at[h, a, pl.ds(0, ROWS)], KV.at[h, a, pl.ds(0, ROWS)], n_ss.at[h, a], n_rs.at[h, a],
                    device_id=dev(z, i + 1 - 2 * core), device_id_type=MESH).wait_recv()

        @pl.when(h == 4)
        def _():
            for kind in (2, 3):
                for d in (1, 2, 3):
                    plane_arrived(d, kind).wait_recv()

            @pl.when(zpar == 1)
            def _():
                for s in range(4):
                    prev_arrived(s).wait_recv()

        parity = jnp.where(h < 4, core, zpar)

        @pl.when(parity == 1)
        def _():
            tiles(h, True)

        @pl.when(parity == 0)
        def _():
            tiles(h, False)

        @pl.when(h == 0)
        def _():
            for kind in (0, 1):
                for d in (1, 2, 3):
                    plane_arrived(d, kind).wait_recv()

        @pl.when((h >= 1) & (h <= nfwd))
        def _():
            forward(h - 1, (z + planes - h) % planes).wait_recv()

        @pl.when((h >= 1) & (h <= nbwd))
        def _():
            backward(h - 1, (z + h) % planes).wait_recv()

        @pl.when(h < nfwd)
        def _():
            forward(h, (z + planes - h) % planes).start()

        @pl.when(h < nbwd)
        def _():
            backward(h, (z + h) % planes).start()

        return carry

    lax.fori_loop(0, HEADS + 1, level_step, 0)

    far_pieces = [(FKV[j, 0], FKV[j, 1], TILE * (z - j)) for j in range(planes)]
    far = softmax_pieces(FQ[...], far_pieces)
    picked = (4, pl.ds(x, 256, stride=4), slice(None))
    mid = (ACC[picked], PK[picked], TT[picked])
    ACC[picked], PK[picked], TT[picked] = merge(mid, far)

    lane = lax.broadcasted_iota(jnp.int32, (256, DH), 1)
    for s in range(4):
        rows = slice(s * 256, (s + 1) * 256)
        total = TT[4, rows, :]
        OB[s] = (ACC[4, rows, :] / total).astype(bf16)
        both = jnp.where(lane == 0, PK[4, rows, :], total)
        ST[s] = jnp.transpose(both)[:8, :]

    def back_copy(d, kind):
        s = plane_peer(d)
        src, dst = ((OB, RO), (ST, RST))[kind]
        return pltpu.make_async_remote_copy(
            src.at[s], dst.at[i], r_ss.at[d - 1, kind], r_rs.at[d - 1, kind],
            device_id=dev(z, s), device_id_type=MESH)

    def back_arrived(d, kind):
        s = (i + 4 - d) % 4
        src, dst = ((OB, RO), (ST, RST))[kind]
        return pltpu.make_async_remote_copy(
            src.at[i], dst.at[s], r_ss.at[d - 1, kind], r_rs.at[d - 1, kind],
            device_id=dev(z, s), device_id_type=MESH)

    for d in (2, 3, 1):
        for kind in range(2):
            back_copy(d, kind).start()
    RO[i] = OB[i]
    RST[i] = ST[i]

    for d in (1, 3, 2):
        for yr in range(2):
            w_arrived(d, yr).wait_recv()
            w_forward(d, yr).start()

    for d in (1, 2, 3):
        for kind in range(2):
            back_arrived(d, kind).wait_recv()
    for s in range(HEADS):
        stats = jnp.transpose(RST[s])
        peak = jnp.broadcast_to(stats[:, 0:1], (256, DH))
        total = jnp.broadcast_to(stats[:, 1:2], (256, DH))
        picked = (s, pl.ds(s, 256, stride=4), slice(None))
        near = (ACC[picked], PK[picked], TT[picked])
        numer, _, whole = merge(near, (RO[s].astype(f32) * total, peak, total))
        ACC[picked] = numer
        TT[picked] = whole
        att_ref[:, s * DH:(s + 1) * DH] = (ACC[s] / TT[s]).astype(bf16)

    for d in (1, 2, 3):
        for yr in range(2):
            w_copy(d, yr).wait_send()
            w_forward(d, yr).wait_send()
            w_forwarded(d, yr).wait_recv()
        for kind in range(4):
            plane_copy(d, kind).wait_send()
        for kind in range(2):
            back_copy(d, kind).wait_send()
    for yr in range(2):
        w_own(yr).wait()
    for hop in range(nfwd):
        forward(hop, (z + planes - hop) % planes).wait_send()
    for hop in range(nbwd):
        backward(hop, (z + hop) % planes).wait_send()

    @pl.when(zpar == 0)
    def _():
        for s in range(4):
            prev_copy(s).wait_send()

    @pl.when(core == 0)
    def _():
        for h in range(HEADS):
            for a in range(2):
                near_copy(h, a).wait_send()


def project_kernel(
    att_ref, wg_ref, out_ref, AL, AR, AO, PS, PR, OWN, OTH,
    r_ss, r_rs, l_ss, l_rs, or_ss, or_rs, ol_ss, ol_rs, y_ss, y_rs,
):
    seq = lax.axis_index("seq")
    head = lax.axis_index("head")
    x = head % 4
    y = head // 4
    right = (seq, y * 4 + (x + 1) % 4)
    left = (seq, y * 4 + (x + 3) % 4)
    across = (seq, (1 - y) * 4 + x)
    steps = ROWS // TILE
    halfrows = TILE // 2

    barrier = pltpu.get_barrier_semaphore()
    for target in (right, left, across):
        pl.semaphore_signal(barrier, inc=1, device_id=target, device_id_type=MESH)
    pl.semaphore_wait(barrier, 3)

    def rows_of(t):
        return pl.ds(pl.multiple_of(t * TILE, TILE), TILE)

    def to_right(t):
        return pltpu.make_async_remote_copy(
            att_ref.at[rows_of(t)], AL.at[rows_of(t)], r_ss.at[t], r_rs.at[t], device_id=right, device_id_type=MESH)

    def to_left(t):
        return pltpu.make_async_remote_copy(
            att_ref.at[rows_of(t)], AR.at[rows_of(t)], l_ss.at[t], l_rs.at[t], device_id=left, device_id_type=MESH)

    def relay_right(t):
        part = pl.ds(pl.multiple_of(t * TILE, halfrows), halfrows)
        return pltpu.make_async_remote_copy(
            AL.at[part], AO.at[part], or_ss.at[t], or_rs.at[t], device_id=right, device_id_type=MESH)

    def relay_left(t):
        part = pl.ds(pl.multiple_of(t * TILE + halfrows, halfrows), halfrows)
        return pltpu.make_async_remote_copy(
            AR.at[part], AO.at[part], ol_ss.at[t], ol_rs.at[t], device_id=left, device_id_type=MESH)

    def to_across(t):
        return pltpu.make_async_remote_copy(
            PS.at[rows_of(t)], PR.at[rows_of(t)], y_ss.at[t], y_rs.at[t], device_id=across, device_id_type=MESH)

    def start_tile(t):
        to_right(t).start()
        to_left(t).start()

    def mm(a, yr, xi):
        return jnp.dot(a, wg_ref[yr, xi], preferred_element_type=f32)

    def finish(t):
        relay_right(t).wait_recv()
        relay_left(t).wait_recv()
        far = AO[rows_of(t), :]
        PS[rows_of(t), :] = (OTH[rows_of(t), :] + mm(far, 1, (x + 2) % 4)).astype(bf16)
        to_across(t).start()
        OWN[rows_of(t), :] = OWN[rows_of(t), :] + mm(far, 0, (x + 2) % 4)

    start_tile(0)
    start_tile(1)

    def step(t, carry):
        to_right(t).wait_recv()
        relay_right(t).start()
        to_left(t).wait_recv()
        relay_left(t).start()

        @pl.when(t + 2 < steps)
        def _():
            start_tile(t + 2)

        here, from_left, from_right = att_ref[rows_of(t), :], AL[rows_of(t), :], AR[rows_of(t), :]
        for yr, acc in ((1, OTH), (0, OWN)):
            acc[rows_of(t), :] = (
                mm(here, yr, x) + mm(from_left, yr, (x + 3) % 4) + mm(from_right, yr, (x + 1) % 4))

        @pl.when(t >= 1)
        def _():
            finish(t - 1)

        return carry

    lax.fori_loop(0, steps, step, 0)
    finish(steps - 1)

    def close(t, carry):
        to_across(t).wait_recv()
        out_ref[rows_of(t), :] = (OWN[rows_of(t), :] + PR[rows_of(t), :].astype(f32)).astype(bf16)
        to_right(t).wait_send()
        to_left(t).wait_send()
        relay_right(t).wait_send()
        relay_left(t).wait_send()
        to_across(t).wait_send()
        return carry

    lax.fori_loop(0, steps, close, 0)


def shards(planes, queries, keys, values, out_weight):
    dma = pltpu.SemaphoreType.DMA
    vmem = pltpu.VMEM
    anywhere = pl.BlockSpec(memory_space=pl.ANY)
    inside = pl.BlockSpec(memory_space=pltpu.VMEM)
    attended, weight = pl.pallas_call(
        functools.partial(attend_kernel, planes),
        name="attend",
        out_shape=(
            jax.ShapeDtypeStruct((ROWS, HEADS * DH), bf16),
            jax.ShapeDtypeStruct((2, 4, 512, 512), bf16),
        ),
        in_specs=[anywhere] * 4,
        out_specs=(inside, anywhere),
        scratch_shapes=[
            vmem((5, ROWS, DH), bf16),
            vmem((5, 2, 2 * ROWS, DH), bf16),
            vmem((4, 3, 256, DH), bf16),
            vmem((4, 3, 64, DH), bf16),
            vmem((256, DH), bf16),
            vmem((planes, 2, 256, DH), bf16),
            vmem((5, ROWS, DH), f32),
            vmem((5, ROWS, DH), f32),
            vmem((5, ROWS, DH), f32),
            vmem((3, ROWS, DH), f32),
            vmem((4, 256, DH), bf16),
            vmem((4, 8, 256), f32),
            vmem((4, 256, DH), bf16),
            vmem((4, 8, 256), f32),
            dma((4, 3)), dma((2,)),
            dma((3, 2)), dma((3, 2)), dma((3, 2)), dma((3, 2)),
            dma((4, 2)), dma((4, 2)),
            dma((3, 4)), dma((3, 4)),
            dma((4,)), dma((4,)),
            dma((4,)), dma((4,)), dma((4,)), dma((4,)),
            dma((3, 2)), dma((3, 2)),
        ],
        compiler_params=pltpu.CompilerParams(
            collective_id=0, has_side_effects=True, vmem_limit_bytes=56 * 1024 * 1024),
    )(queries, keys, values, out_weight)
    return pl.pallas_call(
        project_kernel,
        name="project",
        out_shape=jax.ShapeDtypeStruct((ROWS, 512), bf16),
        in_specs=[inside, inside],
        out_specs=inside,
        scratch_shapes=[vmem((ROWS, 512), bf16)] * 5 + [vmem((ROWS, 512), f32)] * 2 + [dma((4,))] * 10,
        compiler_params=pltpu.CompilerParams(
            collective_id=1, has_side_effects=True, vmem_limit_bytes=48 * 1024 * 1024),
    )(attended, weight)


def solution(mesh):
    placed = (P("seq", "head"), P("seq", "head"), P("seq", "head"), P("head", None))
    planes = mesh.shape["seq"] // 4
    return jax.shard_map(
        functools.partial(shards, planes), mesh=mesh, in_specs=placed, out_specs=P("seq", "head"), check_vma=False
    )
```

time: 338 us -> 103 us (0.30)
  waiting for transfers between devices: 150 us -> 0 us
  Pallas kernels: 0 us -> 101 us
  matrix products: 58.6 us -> 0 us
  other arithmetic: 50.6 us -> 0 us
  local copies, waits for them, and re-layouts: 35.6 us -> 2.19 us
  starting transfers between devices: 25 us -> 0 us
  between operations: 13.5 us -> 0.03 us
    reduce_scatter x1 -> x0, waiting for transfers between devices: 125 us -> none  [shards(): lax.psum_scatter(terms.astype(jnp.bfloat16), 'head', scatter_dimension=1,...]
    pallas_call x0 -> x2, Pallas kernels: none -> 101 us  [the longest x1 51.4 us: shards(): pl.pallas_call(project_kernel, name='project', out_shape=jax.ShapeDtypeSt...]
    dot_general x13 -> x0, matrix products: 58.6 us -> none  [the longest x5 25.2 us: attend_block(): jnp.einsum('hqk,khd->hqd', weights.astype(jnp.bfloat16), value_rows, pref...]
    reduce_sum x8 -> x0, other arithmetic: 30.6 us -> none  [the longest x5 20.3 us: attend_block(): total = jnp.sum(weights, axis=-1)]
    ppermute x8 -> x0, waiting for transfers between devices: 25.1 us -> none  [passed_along(): lax.ppermute(value, axis, [(source, source + steps) for source in range(l...]
    ppermute x8 -> x0, starting transfers between devices: 24.9 us -> none  [passed_along(): lax.ppermute(value, axis, [(source, source + steps) for source in range(l...]
    concatenate x6 -> x0, other arithmetic: 12.4 us -> none  [the longest x2 4.03 us: shards(): block_values = jnp.concatenate([moved[1], block_values], axis=0)]
    concatenate x6 -> x0, local copies, waits for them, and re-layouts: 9.82 us -> none  [the longest x3 5.58 us: shards(): block_values = jnp.concatenate([moved[1], block_values], axis=0)]
  transfers between devices with their start and end apart: 11 -> 0, of which waited for: 4 -> 0; matrix products, arithmetic and copies ran while one was open for 34% -> 0% of each run, Pallas kernels for 0% -> 0%
where the time goes in v1:
time: 103 us
  Pallas kernels  101 us (98%)
  local copies, waits for them, and re-layouts  2.19 us (2%)
    pallas_call x1, Pallas kernels, shards(): pl.pallas_call(project_kernel, name='project', out_shape=jax.ShapeDtypeSt...  51.4 us
    pallas_call x1, Pallas kernels, shards(): pl.pallas_call(functools.partial(attend_kernel, planes), name='attend', o...  49.6 us
    unnamed x3, local copies, waits for them, and re-layouts  2.19 us

profile of v1, /device:TPU:1, one launch (start us, length us, event | category | flops | bytes accessed | tf_op | source)
XLA Modules:
  0.0 103.1 jit_solution(16374625088255266982)
XLA Ops:
  0.0 49.6 %attend.1 = (bf16[1024,512]{1,0:T(8,128)(2,1)}, bf16[2,4,512,512]{3,2,1,0:T(8,128)(2,1)}) custom-call(bf16[1024,512]{1,0:T(8,128)(2,1)} %q_hbm.1, bf16[1024,512]{1,0:T(8,128)(2,1)} %k_hbm.1, bf16[1024,512]{1,0:T(8,128)(2,1)} %v_hbm.1, bf16[512,4096]{1,0:T(8,128)(2,1)} %w_hbm.1), custom_call_target="tpu_custom_call" | custom-call | tf_op jit(solution)/shard_map/attend/pallas_call | solution.py:490
  49.6 0.0 copy-start
  49.6 1.2 %copy-done = bf16[1024,512]{1,0:T(8,128)(2,1)S(1)} copy-done((bf16[1024,512]{1,0:T(8,128)(2,1)S(1)}, bf16[1024,512]{1,0:T(8,128)(2,1)}, u32[]{:S(2)}) %copy-start) | copy-done | bytes 1048600
  50.8 51.4 %project.1 = bf16[1024,512]{1,0:T(8,128)(2,1)S(1)} custom-call(bf16[1024,512]{1,0:T(8,128)(2,1)S(1)} %copy-done, bf16[2,4,512,512]{3,2,1,0:T(8,128)(2,1)} %get-tuple-element.8.wg_ref), custom_call_target="tpu_custom_call" | custom-call | tf_op jit(solution)/shard_map/project/pallas_call | solution.py:525
  102.2 1.0 copy.6
Async XLA Ops:
  49.6 1.2 %copy-start = (bf16[1024,512]{1,0:T(8,128)(2,1)S(1)}, bf16[1024,512]{1,0:T(8,128)(2,1)}, u32[]{:S(2)}) copy-start(bf16[1024,512]{1,0:T(8,128)(2,1)} %get-tuple-element.7.att_ref) | copy-start | bytes 3145732

commit v2 on v1

--- a/solution.py
+++ b/solution.py
@@ -52,12 +52,13 @@
     return numer1 * f1 + numer2 * f2, top, total1 * f1 + total2 * f2
 
 
-def attend_kernel(
+def layer_kernel(
     planes,
-    q_hbm, k_hbm, v_hbm, w_hbm, att_ref, wg_ref,
-    QA, KV, SM, SF, FQ, FKV, ACC, PK, TT, TMP, RO, RST, OB, ST,
-    loc, locw, w_ss, w_rs, wf_ss, wf_rs, n_ss, n_rs, p_ss, p_rs, pv_ss, pv_rs,
-    f_ss, f_rs, b_ss, b_rs, r_ss, r_rs,
+    q_hbm, k_hbm, v_hbm, w_hbm, out_ref,
+    QA, KV, SM, SF, FQ, FKV, ACC, PK, TT, TMP, RO, RST, OB, ST, CQ, WG, AG, PS, PR, OWN, OTH,
+    loc, locw, w_ss, w_rs, wf_ss, wf_rs, n_ss, n_rs, p_ss, p_rs, cq_ss, cq_rs,
+    f_ss, f_rs, b_ss, b_rs, r_ss, r_rs, cr_ss, cr_rs,
+    ar_ss, ar_rs, al_ss, al_rs, or_ss, or_rs, ol_ss, ol_rs, y_ss, y_rs,
 ):
     seq = lax.axis_index("seq")
     head = lax.axis_index("head")
@@ -90,11 +91,22 @@
         for copy in loads[-1]:
             copy.start()
 
+    def w_own(yr):
+        col = pl.multiple_of((((y + yr) % 2) * 4 + x) * 512, 512)
+        return pltpu.make_async_copy(w_hbm.at[:, pl.ds(col, 512)], WG.at[yr, x], locw.at[yr])
+
+    for yr in range(2):
+        w_own(yr).start()
+
     barrier = pltpu.get_barrier_semaphore()
     greet = [dev(z, plane_peer(d)) for d in (1, 2, 3)]
     greet += [dev(pair, s) for s in range(4)]
     greet += [dev(zother, i)]
     greet += [(seq, y * 4 + (x + d) % 4) for d in (1, 2, 3)]
+    right = (seq, y * 4 + (x + 1) % 4)
+    left = (seq, y * 4 + (x + 3) % 4)
+    across = (seq, (1 - y) * 4 + x)
+    greet += [across]
     for target in greet:
         pl.semaphore_signal(barrier, inc=1, device_id=target, device_id_type=MESH)
     pl.semaphore_wait(barrier, len(greet))
@@ -119,23 +131,23 @@
         col = pl.multiple_of((yd * 4 + xd) * 512, 512)
         return pltpu.make_async_remote_copy(
             w_hbm.at[pl.ds(half, 256), pl.ds(col, 512)],
-            wg_ref.at[yr, x, pl.ds(half, 256)],
+            WG.at[yr, x, pl.ds(half, 256)],
             w_ss.at[d - 1, yr], w_rs.at[d - 1, yr],
             device_id=(seq, y * 4 + xd), device_id_type=MESH)
 
     def w_arrived(d, yr):
         xs = (x + 4 - d) % 4
         return pltpu.make_async_remote_copy(
-            wg_ref.at[yr, xs, pl.ds(half, 256)],
-            wg_ref.at[yr, xs, pl.ds(half, 256)],
+            WG.at[yr, xs, pl.ds(half, 256)],
+            WG.at[yr, xs, pl.ds(half, 256)],
             w_ss.at[d - 1, yr], w_rs.at[d - 1, yr],
             device_id=(seq, y * 4 + xs), device_id_type=MESH)
 
     def w_forward(d, yr):
         xs = (x + 4 - d) % 4
         return pltpu.make_async_remote_copy(
-            wg_ref.at[yr, xs, pl.ds(half, 256)],
-            wg_ref.at[yr, xs, pl.ds(half, 256)],
+            WG.at[yr, xs, pl.ds(half, 256)],
+            WG.at[yr, xs, pl.ds(half, 256)],
             wf_ss.at[d - 1, yr], wf_rs.at[d - 1, yr],
             device_id=dev(z, i + 1 - 2 * core), device_id_type=MESH)
 
@@ -143,21 +155,14 @@
         xs = (x + 4 - d) % 4
         other = pl.multiple_of(256 - half, 256)
         return pltpu.make_async_remote_copy(
-            wg_ref.at[yr, xs, pl.ds(other, 256)],
-            wg_ref.at[yr, xs, pl.ds(other, 256)],
+            WG.at[yr, xs, pl.ds(other, 256)],
+            WG.at[yr, xs, pl.ds(other, 256)],
             wf_ss.at[d - 1, yr], wf_rs.at[d - 1, yr],
             device_id=dev(z, i + 1 - 2 * core), device_id_type=MESH)
 
     for d in (1, 3, 2):
         for yr in range(2):
             w_copy(d, yr).start()
-
-    def w_own(yr):
-        col = pl.multiple_of((((y + yr) % 2) * 4 + x) * 512, 512)
-        return pltpu.make_async_copy(w_hbm.at[:, pl.ds(col, 512)], wg_ref.at[yr, x], locw.at[yr])
-
-    for yr in range(2):
-        w_own(yr).start()
 
     for h in range(HEADS):
         for a in range(3):
@@ -188,28 +193,23 @@
             src, dst, p_ss.at[d - 1, kind], p_rs.at[d - 1, kind],
             device_id=dev(z, target), device_id_type=MESH)
 
-    def prev_copy(s):
-        return pltpu.make_async_remote_copy(
-            SM.at[s, pl.ds(1, 2)], KV.at[4, :, pl.ds(pl.multiple_of(i * 256, 256), 256)],
-            pv_ss.at[s], pv_rs.at[i], device_id=dev(pair, s), device_id_type=MESH)
-
-    def prev_arrived(s):
-        return pltpu.make_async_remote_copy(
-            SM.at[s, pl.ds(1, 2)], KV.at[4, :, pl.ds(s * 256, 256)],
-            pv_ss.at[s], pv_rs.at[s], device_id=dev(pair, s), device_id_type=MESH)
+    def cross_query(s, sender):
+        return pltpu.make_async_remote_copy(
+            SM.at[s, 0], CQ.at[pl.ds(pl.multiple_of(sender * 256, 256), 256)],
+            cq_ss.at[s], cq_rs.at[sender], device_id=dev(pair, s), device_id_type=MESH)
 
     for kind in (0, 1):
         for d in (2, 3, 1):
             plane_copy(d, kind).start()
 
-    @pl.when(zpar == 0)
-    def _():
-        for s in range(4):
-            prev_copy(s).start()
-
     for kind in (2, 3):
         for d in (2, 3, 1):
             plane_copy(d, kind).start()
+
+    @pl.when(zpar == 1)
+    def _():
+        for s in range(4):
+            cross_query(s, i).start()
 
     own_mid = pl.multiple_of(i * 256, 256)
     own_far = pl.multiple_of(i * 64, 64)
@@ -244,6 +244,39 @@
             PK[h, rows, :] = peak
             TT[h, rows, :] = total
 
+    def x_copy(part, sem):
+        return (
+            pltpu.make_async_remote_copy(
+                AG.at[(0,) + part], AG.at[(1,) + part], ar_ss.at[sem], ar_rs.at[sem],
+                device_id=right, device_id_type=MESH),
+            pltpu.make_async_remote_copy(
+                AG.at[(0,) + part], AG.at[(3,) + part], al_ss.at[sem], al_rs.at[sem],
+                device_id=left, device_id_type=MESH),
+        )
+
+    def x_relay(part, sem):
+        top = part + (pl.ds(0, 128),)
+        low = part + (pl.ds(128, 128),)
+        return (
+            pltpu.make_async_remote_copy(
+                AG.at[(1,) + top], AG.at[(2,) + top], or_ss.at[sem], or_rs.at[sem],
+                device_id=right, device_id_type=MESH),
+            pltpu.make_async_remote_copy(
+                AG.at[(3,) + low], AG.at[(2,) + low], ol_ss.at[sem], ol_rs.at[sem],
+                device_id=left, device_id_type=MESH),
+        )
+
+    def x_pass_on(part, sem):
+        for arrived, onward in zip(x_copy(part, sem), x_relay(part, sem)):
+            arrived.wait_recv()
+            onward.start()
+
+    def near_part(h):
+        return (h, pl.ds(1, 3))
+
+    def strided_part(h):
+        return (h, 0)
+
     nfwd = planes // 2
     nbwd = planes - 1 - nfwd
 
@@ -261,12 +294,7 @@
                 for d in (1, 2, 3):
                     plane_arrived(d, kind).wait_recv()
 
-            @pl.when(zpar == 1)
-            def _():
-                for s in range(4):
-                    prev_arrived(s).wait_recv()
-
-        parity = jnp.where(h < 4, core, zpar)
+        parity = jnp.where(h < 4, core, 0)
 
         @pl.when(parity == 1)
         def _():
@@ -298,23 +326,47 @@
         def _():
             backward(h, (z + h) % planes).start()
 
+        @pl.when(h < 4)
+        def _():
+            for rr in range(1, 4):
+                picked = (h, pl.ds((h + rr) % 4, 256, stride=4), slice(None))
+                AG[0, h, rr] = (ACC[picked] / TT[picked]).astype(bf16)
+            for copy in x_copy(near_part(h), h):
+                copy.start()
+
         return carry
 
     lax.fori_loop(0, HEADS + 1, level_step, 0)
+
+    lane = lax.broadcasted_iota(jnp.int32, (256, DH), 1)
+
+    def pack(slot, numer, peak, total):
+        OB[slot] = (numer / total).astype(bf16)
+        ST[slot] = jnp.transpose(jnp.where(lane == 0, peak, total))[:8, :]
+
+    def cross_result(s, sender, kind):
+        src, dst = ((OB, RO), (ST, RST))[kind]
+        return pltpu.make_async_remote_copy(
+            src.at[4 + s], dst.at[4 + sender], cr_ss.at[s, kind], cr_rs.at[sender, kind],
+            device_id=dev(pair, s), device_id_type=MESH)
+
+    @pl.when(zpar == 0)
+    def _():
+        for s in range(4):
+            cross_query(s, s).wait_recv()
+            rows = slice(s * 256, (s + 1) * 256)
+            pack(4 + s, *softmax_pieces(CQ[rows, :], [(KV[4, 0, ROWS:, :], KV[4, 1, ROWS:, :], None)]))
+            for kind in range(2):
+                cross_result(s, i, kind).start()
 
     far_pieces = [(FKV[j, 0], FKV[j, 1], TILE * (z - j)) for j in range(planes)]
     far = softmax_pieces(FQ[...], far_pieces)
     picked = (4, pl.ds(x, 256, stride=4), slice(None))
     mid = (ACC[picked], PK[picked], TT[picked])
     ACC[picked], PK[picked], TT[picked] = merge(mid, far)
-
-    lane = lax.broadcasted_iota(jnp.int32, (256, DH), 1)
     for s in range(4):
         rows = slice(s * 256, (s + 1) * 256)
-        total = TT[4, rows, :]
-        OB[s] = (ACC[4, rows, :] / total).astype(bf16)
-        both = jnp.where(lane == 0, PK[4, rows, :], total)
-        ST[s] = jnp.transpose(both)[:8, :]
+        pack(s, ACC[4, rows, :], PK[4, rows, :], TT[4, rows, :])
 
     def back_copy(d, kind):
         s = plane_peer(d)
@@ -344,158 +396,127 @@
     for d in (1, 2, 3):
         for kind in range(2):
             back_arrived(d, kind).wait_recv()
-    for s in range(HEADS):
-        stats = jnp.transpose(RST[s])
+
+    @pl.when(zpar == 1)
+    def _():
+        for s in range(4):
+            for kind in range(2):
+                cross_result(s, s, kind).wait_recv()
+
+    def unpack(slot):
+        stats = jnp.transpose(RST[slot])
         peak = jnp.broadcast_to(stats[:, 0:1], (256, DH))
         total = jnp.broadcast_to(stats[:, 1:2], (256, DH))
+        return RO[slot].astype(f32) * total, peak, total
+
+    for s in range(HEADS):
         picked = (s, pl.ds(s, 256, stride=4), slice(None))
-        near = (ACC[picked], PK[picked], TT[picked])
-        numer, _, whole = merge(near, (RO[s].astype(f32) * total, peak, total))
-        ACC[picked] = numer
-        TT[picked] = whole
-        att_ref[:, s * DH:(s + 1) * DH] = (ACC[s] / TT[s]).astype(bf16)
+        state = merge((ACC[picked], PK[picked], TT[picked]), unpack(s))
+
+        @pl.when(zpar == 0)
+        def _():
+            AG[0, s, 0] = (state[0] / state[2]).astype(bf16)
+
+        @pl.when(zpar == 1)
+        def _():
+            numer, _, total = merge(state, unpack(4 + s))
+            AG[0, s, 0] = (numer / total).astype(bf16)
+
+        for copy in x_copy(strided_part(s), 4 + s):
+            copy.start()
+
+    for h in range(HEADS):
+        x_pass_on(near_part(h), h)
+    for d in (1, 2, 3):
+        for yr in range(2):
+            w_forwarded(d, yr).wait_recv()
+    for yr in range(2):
+        w_own(yr).wait()
+
+    def weight(yr, j, h):
+        return WG[yr, (x + 4 - j) % 4, h * DH:(h + 1) * DH, :]
+
+    def product(r, yr, blocks):
+        left_side = jnp.concatenate([AG[j, h, (r - h) % 4] for j, h in blocks], axis=1)
+        right_side = jnp.concatenate([weight(yr, j, h) for j, h in blocks], axis=0)
+        return jnp.dot(left_side, right_side, preferred_element_type=f32)
+
+    for r in range(4):
+        blocks = [(j, h) for j in (0, 1, 3) for h in range(HEADS) if h != r]
+        for yr, acc in ((1, OTH), (0, OWN)):
+            acc[r] = product(r, yr, blocks)
+
+    def to_across(r):
+        return pltpu.make_async_remote_copy(
+            PS.at[r], PR.at[r], y_ss.at[r], y_rs.at[r], device_id=across, device_id_type=MESH)
+
+    for h in range(HEADS):
+        x_pass_on(strided_part(h), 4 + h)
+    for h in range(HEADS):
+        for copy in x_relay(near_part(h), h):
+            copy.wait_recv()
+    for r in range(4):
+        for copy in x_relay(strided_part(r), 4 + r):
+            copy.wait_recv()
+        blocks = [(2, h) for h in range(HEADS) if h != r] + [(j, r) for j in range(4)]
+        PS[r] = (OTH[r] + product(r, 1, blocks)).astype(bf16)
+        to_across(r).start()
+        OWN[r] = OWN[r] + product(r, 0, blocks)
+
+    for r in range(4):
+        to_across(r).wait_recv()
+        mixed = OWN[r] + PR[r].astype(f32)
+        for c in range(4):
+            ACC[c, pl.ds(r, 256, stride=4), :] = mixed[:, c * DH:(c + 1) * DH]
+    for c in range(4):
+        out_ref[:, c * DH:(c + 1) * DH] = ACC[c].astype(bf16)
 
     for d in (1, 2, 3):
         for yr in range(2):
             w_copy(d, yr).wait_send()
             w_forward(d, yr).wait_send()
-            w_forwarded(d, yr).wait_recv()
         for kind in range(4):
             plane_copy(d, kind).wait_send()
         for kind in range(2):
             back_copy(d, kind).wait_send()
-    for yr in range(2):
-        w_own(yr).wait()
     for hop in range(nfwd):
         forward(hop, (z + planes - hop) % planes).wait_send()
     for hop in range(nbwd):
         backward(hop, (z + hop) % planes).wait_send()
+    for h in range(HEADS):
+        for part, sem in ((near_part(h), h), (strided_part(h), 4 + h)):
+            for copy in x_copy(part, sem) + x_relay(part, sem):
+                copy.wait_send()
+        to_across(h).wait_send()
+
+    @pl.when(zpar == 1)
+    def _():
+        for s in range(4):
+            cross_query(s, i).wait_send()
 
     @pl.when(zpar == 0)
     def _():
         for s in range(4):
-            prev_copy(s).wait_send()
+            for kind in range(2):
+                cross_result(s, i, kind).wait_send()
 
     @pl.when(core == 0)
     def _():
         for h in range(HEADS):
             for a in range(2):
                 near_copy(h, a).wait_send()
-
-
-def project_kernel(
-    att_ref, wg_ref, out_ref, AL, AR, AO, PS, PR, OWN, OTH,
-    r_ss, r_rs, l_ss, l_rs, or_ss, or_rs, ol_ss, ol_rs, y_ss, y_rs,
-):
-    seq = lax.axis_index("seq")
-    head = lax.axis_index("head")
-    x = head % 4
-    y = head // 4
-    right = (seq, y * 4 + (x + 1) % 4)
-    left = (seq, y * 4 + (x + 3) % 4)
-    across = (seq, (1 - y) * 4 + x)
-    steps = ROWS // TILE
-    halfrows = TILE // 2
-
-    barrier = pltpu.get_barrier_semaphore()
-    for target in (right, left, across):
-        pl.semaphore_signal(barrier, inc=1, device_id=target, device_id_type=MESH)
-    pl.semaphore_wait(barrier, 3)
-
-    def rows_of(t):
-        return pl.ds(pl.multiple_of(t * TILE, TILE), TILE)
-
-    def to_right(t):
-        return pltpu.make_async_remote_copy(
-            att_ref.at[rows_of(t)], AL.at[rows_of(t)], r_ss.at[t], r_rs.at[t], device_id=right, device_id_type=MESH)
-
-    def to_left(t):
-        return pltpu.make_async_remote_copy(
-            att_ref.at[rows_of(t)], AR.at[rows_of(t)], l_ss.at[t], l_rs.at[t], device_id=left, device_id_type=MESH)
-
-    def relay_right(t):
-        part = pl.ds(pl.multiple_of(t * TILE, halfrows), halfrows)
-        return pltpu.make_async_remote_copy(
-            AL.at[part], AO.at[part], or_ss.at[t], or_rs.at[t], device_id=right, device_id_type=MESH)
-
-    def relay_left(t):
-        part = pl.ds(pl.multiple_of(t * TILE + halfrows, halfrows), halfrows)
-        return pltpu.make_async_remote_copy(
-            AR.at[part], AO.at[part], ol_ss.at[t], ol_rs.at[t], device_id=left, device_id_type=MESH)
-
-    def to_across(t):
-        return pltpu.make_async_remote_copy(
-            PS.at[rows_of(t)], PR.at[rows_of(t)], y_ss.at[t], y_rs.at[t], device_id=across, device_id_type=MESH)
-
-    def start_tile(t):
-        to_right(t).start()
-        to_left(t).start()
-
-    def mm(a, yr, xi):
-        return jnp.dot(a, wg_ref[yr, xi], preferred_element_type=f32)
-
-    def finish(t):
-        relay_right(t).wait_recv()
-        relay_left(t).wait_recv()
-        far = AO[rows_of(t), :]
-        PS[rows_of(t), :] = (OTH[rows_of(t), :] + mm(far, 1, (x + 2) % 4)).astype(bf16)
-        to_across(t).start()
-        OWN[rows_of(t), :] = OWN[rows_of(t), :] + mm(far, 0, (x + 2) % 4)
-
-    start_tile(0)
-    start_tile(1)
-
-    def step(t, carry):
-        to_right(t).wait_recv()
-        relay_right(t).start()
-        to_left(t).wait_recv()
-        relay_left(t).start()
-
-        @pl.when(t + 2 < steps)
-        def _():
-            start_tile(t + 2)
-
-        here, from_left, from_right = att_ref[rows_of(t), :], AL[rows_of(t), :], AR[rows_of(t), :]
-        for yr, acc in ((1, OTH), (0, OWN)):
-            acc[rows_of(t), :] = (
-                mm(here, yr, x) + mm(from_left, yr, (x + 3) % 4) + mm(from_right, yr, (x + 1) % 4))
-
-        @pl.when(t >= 1)
-        def _():
-            finish(t - 1)
-
-        return carry
-
-    lax.fori_loop(0, steps, step, 0)
-    finish(steps - 1)
-
-    def close(t, carry):
-        to_across(t).wait_recv()
-        out_ref[rows_of(t), :] = (OWN[rows_of(t), :] + PR[rows_of(t), :].astype(f32)).astype(bf16)
-        to_right(t).wait_send()
-        to_left(t).wait_send()
-        relay_right(t).wait_send()
-        relay_left(t).wait_send()
-        to_across(t).wait_send()
-        return carry
-
-    lax.fori_loop(0, steps, close, 0)
 
 
 def shards(planes, queries, keys, values, out_weight):
     dma = pltpu.SemaphoreType.DMA
     vmem = pltpu.VMEM
     anywhere = pl.BlockSpec(memory_space=pl.ANY)
-    inside = pl.BlockSpec(memory_space=pltpu.VMEM)
-    attended, weight = pl.pallas_call(
-        functools.partial(attend_kernel, planes),
-        name="attend",
-        out_shape=(
-            jax.ShapeDtypeStruct((ROWS, HEADS * DH), bf16),
-            jax.ShapeDtypeStruct((2, 4, 512, 512), bf16),
-        ),
+    return pl.pallas_call(
+        functools.partial(layer_kernel, planes),
+        name="layer",
+        out_shape=jax.ShapeDtypeStruct((ROWS, HEADS * DH), bf16),
         in_specs=[anywhere] * 4,
-        out_specs=(inside, anywhere),
+        out_specs=pl.BlockSpec(memory_space=pltpu.VMEM),
         scratch_shapes=[
             vmem((5, ROWS, DH), bf16),
             vmem((5, 2, 2 * ROWS, DH), bf16),
@@ -507,10 +528,17 @@
             vmem((5, ROWS, DH), f32),
             vmem((5, ROWS, DH), f32),
             vmem((3, ROWS, DH), f32),
-            vmem((4, 256, DH), bf16),
-            vmem((4, 8, 256), f32),
-            vmem((4, 256, DH), bf16),
-            vmem((4, 8, 256), f32),
+            vmem((8, 256, DH), bf16),
+            vmem((8, 8, 256), f32),
+            vmem((8, 256, DH), bf16),
+            vmem((8, 8, 256), f32),
+            vmem((ROWS, DH), bf16),
+            vmem((2, 4, 512, 512), bf16),
+            vmem((4, 4, 4, 256, DH), bf16),
+            vmem((4, 256, 512), bf16),
+            vmem((4, 256, 512), bf16),
+            vmem((4, 256, 512), f32),
+            vmem((4, 256, 512), f32),
             dma((4, 3)), dma((2,)),
             dma((3, 2)), dma((3, 2)), dma((3, 2)), dma((3, 2)),
             dma((4, 2)), dma((4, 2)),
@@ -518,20 +546,11 @@
             dma((4,)), dma((4,)),
             dma((4,)), dma((4,)), dma((4,)), dma((4,)),
             dma((3, 2)), dma((3, 2)),
-        ],
+            dma((4, 2)), dma((4, 2)),
+        ] + [dma((8,))] * 8 + [dma((4,))] * 2,
         compiler_params=pltpu.CompilerParams(
-            collective_id=0, has_side_effects=True, vmem_limit_bytes=56 * 1024 * 1024),
+            collective_id=0, has_side_effects=True, vmem_limit_bytes=58 * 1024 * 1024),
     )(queries, keys, values, out_weight)
-    return pl.pallas_call(
-        project_kernel,
-        name="project",
-        out_shape=jax.ShapeDtypeStruct((ROWS, 512), bf16),
-        in_specs=[inside, inside],
-        out_specs=inside,
-        scratch_shapes=[vmem((ROWS, 512), bf16)] * 5 + [vmem((ROWS, 512), f32)] * 2 + [dma((4,))] * 10,
-        compiler_params=pltpu.CompilerParams(
-            collective_id=1, has_side_effects=True, vmem_limit_bytes=48 * 1024 * 1024),
-    )(attended, weight)
 
 
 def solution(mesh):

time: 103 us -> 94.3 us (0.916); the launches traced: 103 us -> 93.3 us
  Pallas kernels: 101 us -> 91 us
    pallas_call x2 -> x1, Pallas kernels: 101 us -> 91 us  [shards(): pl.pallas_call(functools.partial(layer_kernel, planes), name='layer', out...]
    unnamed x3 -> x1, local copies, waits for them, and re-layouts: 2.19 us -> 2.26 us
where the time goes in v2:
time: 94.3 us; the launch traced here: 93.3 us
  Pallas kernels  91 us (97%)
  local copies, waits for them, and re-layouts  2.26 us (2%)
    pallas_call x1, Pallas kernels, shards(): pl.pallas_call(functools.partial(layer_kernel, planes), name='layer', out...  91 us
    unnamed x1, local copies, waits for them, and re-layouts  2.26 us

profile of v2, /device:TPU:1, one launch (start us, length us, event | category | flops | bytes accessed | tf_op | source)
XLA Modules:
  0.0 93.3 jit_solution(6359752849906315724)
XLA Ops:
  0.0 91.0 %layer.1 = bf16[1024,512]{1,0:T(8,128)(2,1)} custom-call(bf16[1024,512]{1,0:T(8,128)(2,1)} %q_hbm.1, bf16[1024,512]{1,0:T(8,128)(2,1)} %k_hbm.1, bf16[1024,512]{1,0:T(8,128)(2,1)} %v_hbm.1, bf16[512,4096]{1,0:T(8,128)(2,1)} %w_hbm.1), custom_call_target="tpu_custom_call" | custom-call | tf_op jit(solution)/shard_map/layer/pallas_call | solution.py:514
  91.1 2.3 %copy.6 = bf16[1024,512]{1,0:T(8,128)(2,1)} copy(bf16[1024,512]{1,0:T(8,128)(2,1)} %layer.1) | data formatting | bytes 2097152

commit v3 on v2

--- a/solution.py
+++ b/solution.py
@@ -56,7 +56,7 @@
     planes,
     q_hbm, k_hbm, v_hbm, w_hbm, out_ref,
     QA, KV, SM, SF, FQ, FKV, ACC, PK, TT, TMP, RO, RST, OB, ST, CQ, WG, AG, PS, PR, OWN, OTH,
-    loc, locw, w_ss, w_rs, wf_ss, wf_rs, n_ss, n_rs, p_ss, p_rs, cq_ss, cq_rs,
+    loc, locw, w_ss, w_rs, wy_ss, wy_rs, wf_ss, wf_rs, wg_ss, wg_rs, n_ss, n_rs, p_ss, p_rs, cq_ss, cq_rs,
     f_ss, f_rs, b_ss, b_rs, r_ss, r_rs, cr_ss, cr_rs,
     ar_ss, ar_rs, al_ss, al_rs, or_ss, or_rs, ol_ss, ol_rs, y_ss, y_rs,
 ):
@@ -123,42 +123,47 @@
             for a in range(2):
                 near_copy(h, a).start()
 
-    half = pl.multiple_of(core * 256, 256)
+    chip_mate = i + 1 - 2 * core
+    y_mate = (i + 2) % 4
+
+    def quarter(slot):
+        return pl.ds(pl.multiple_of(slot * 128, 128), 128)
 
     def w_copy(d, yr):
         xd = (x + d) % 4
         yd = (y + yr) % 2
         col = pl.multiple_of((yd * 4 + xd) * 512, 512)
         return pltpu.make_async_remote_copy(
-            w_hbm.at[pl.ds(half, 256), pl.ds(col, 512)],
-            WG.at[yr, x, pl.ds(half, 256)],
+            w_hbm.at[quarter(i), pl.ds(col, 512)], WG.at[yr, x, quarter(i)],
             w_ss.at[d - 1, yr], w_rs.at[d - 1, yr],
             device_id=(seq, y * 4 + xd), device_id_type=MESH)
 
+    def w_share(d, yr, slot, sems, target):
+        piece = WG.at[yr, (x + 4 - d) % 4, quarter(slot)]
+        return pltpu.make_async_remote_copy(
+            piece, piece, sems[0].at[d - 1, yr], sems[1].at[d - 1, yr],
+            device_id=target, device_id_type=MESH)
+
     def w_arrived(d, yr):
-        xs = (x + 4 - d) % 4
-        return pltpu.make_async_remote_copy(
-            WG.at[yr, xs, pl.ds(half, 256)],
-            WG.at[yr, xs, pl.ds(half, 256)],
-            w_ss.at[d - 1, yr], w_rs.at[d - 1, yr],
-            device_id=(seq, y * 4 + xs), device_id_type=MESH)
-
-    def w_forward(d, yr):
-        xs = (x + 4 - d) % 4
-        return pltpu.make_async_remote_copy(
-            WG.at[yr, xs, pl.ds(half, 256)],
-            WG.at[yr, xs, pl.ds(half, 256)],
-            wf_ss.at[d - 1, yr], wf_rs.at[d - 1, yr],
-            device_id=dev(z, i + 1 - 2 * core), device_id_type=MESH)
-
-    def w_forwarded(d, yr):
-        xs = (x + 4 - d) % 4
-        other = pl.multiple_of(256 - half, 256)
-        return pltpu.make_async_remote_copy(
-            WG.at[yr, xs, pl.ds(other, 256)],
-            WG.at[yr, xs, pl.ds(other, 256)],
-            wf_ss.at[d - 1, yr], wf_rs.at[d - 1, yr],
-            device_id=dev(z, i + 1 - 2 * core), device_id_type=MESH)
+        return w_share(d, yr, i, (w_ss, w_rs), (seq, y * 4 + (x + 4 - d) % 4))
+
+    def w_cross(d, yr):
+        return w_share(d, yr, i, (wy_ss, wy_rs), dev(z, y_mate))
+
+    def w_crossed(d, yr):
+        return w_share(d, yr, y_mate, (wy_ss, wy_rs), dev(z, y_mate))
+
+    def w_chip(d, yr):
+        return w_share(d, yr, i, (wf_ss, wf_rs), dev(z, chip_mate))
+
+    def w_chipped(d, yr):
+        return w_share(d, yr, chip_mate, (wf_ss, wf_rs), dev(z, chip_mate))
+
+    def w_last(d, yr):
+        return w_share(d, yr, y_mate, (wg_ss, wg_rs), dev(z, chip_mate))
+
+    def w_lasted(d, yr):
+        return w_share(d, yr, (chip_mate + 2) % 4, (wg_ss, wg_rs), dev(z, chip_mate))
 
     for d in (1, 3, 2):
         for yr in range(2):
@@ -310,6 +315,11 @@
                 for d in (1, 2, 3):
                     plane_arrived(d, kind).wait_recv()
 
+        @pl.when(h == 4)
+        def _():
+            for early in range(2):
+                x_pass_on(near_part(early), early)
+
         @pl.when((h >= 1) & (h <= nfwd))
         def _():
             forward(h - 1, (z + planes - h) % planes).wait_recv()
@@ -333,6 +343,14 @@
                 AG[0, h, rr] = (ACC[picked] / TT[picked]).astype(bf16)
             for copy in x_copy(near_part(h), h):
                 copy.start()
+
+        @pl.when(h == 2)
+        def _():
+            for d in (1, 3, 2):
+                for yr in range(2):
+                    w_arrived(d, yr).wait_recv()
+                    w_cross(d, yr).start()
+                    w_chip(d, yr).start()
 
         return carry
 
@@ -388,10 +406,33 @@
     RO[i] = OB[i]
     RST[i] = ST[i]
 
+    for late in (2, 3):
+        x_pass_on(near_part(late), late)
+
     for d in (1, 3, 2):
         for yr in range(2):
-            w_arrived(d, yr).wait_recv()
-            w_forward(d, yr).start()
+            w_crossed(d, yr).wait_recv()
+            w_last(d, yr).start()
+
+    for d in (1, 2, 3):
+        for yr in range(2):
+            w_chipped(d, yr).wait_recv()
+            w_lasted(d, yr).wait_recv()
+    for yr in range(2):
+        w_own(yr).wait()
+
+    def weight(yr, j, h):
+        return WG[yr, (x + 4 - j) % 4, h * DH:(h + 1) * DH, :]
+
+    def product(r, yr, blocks):
+        left_side = jnp.concatenate([AG[j, h, (r - h) % 4] for j, h in blocks], axis=1)
+        right_side = jnp.concatenate([weight(yr, j, h) for j, h in blocks], axis=0)
+        return jnp.dot(left_side, right_side, preferred_element_type=f32)
+
+    for r in range(4):
+        blocks = [(j, h) for j in (0, 1, 3) for h in range(HEADS) if h != r]
+        for yr, acc in ((1, OTH), (0, OWN)):
+            acc[r] = product(r, yr, blocks)
 
     for d in (1, 2, 3):
         for kind in range(2):
@@ -425,43 +466,27 @@
         for copy in x_copy(strided_part(s), 4 + s):
             copy.start()
 
-    for h in range(HEADS):
-        x_pass_on(near_part(h), h)
-    for d in (1, 2, 3):
-        for yr in range(2):
-            w_forwarded(d, yr).wait_recv()
-    for yr in range(2):
-        w_own(yr).wait()
-
-    def weight(yr, j, h):
-        return WG[yr, (x + 4 - j) % 4, h * DH:(h + 1) * DH, :]
-
-    def product(r, yr, blocks):
-        left_side = jnp.concatenate([AG[j, h, (r - h) % 4] for j, h in blocks], axis=1)
-        right_side = jnp.concatenate([weight(yr, j, h) for j, h in blocks], axis=0)
-        return jnp.dot(left_side, right_side, preferred_element_type=f32)
-
-    for r in range(4):
-        blocks = [(j, h) for j in (0, 1, 3) for h in range(HEADS) if h != r]
-        for yr, acc in ((1, OTH), (0, OWN)):
-            acc[r] = product(r, yr, blocks)
-
     def to_across(r):
         return pltpu.make_async_remote_copy(
             PS.at[r], PR.at[r], y_ss.at[r], y_rs.at[r], device_id=across, device_id_type=MESH)
 
-    for h in range(HEADS):
-        x_pass_on(strided_part(h), 4 + h)
-    for h in range(HEADS):
-        for copy in x_relay(near_part(h), h):
-            copy.wait_recv()
-    for r in range(4):
+    def finish(r):
         for copy in x_relay(strided_part(r), 4 + r):
             copy.wait_recv()
         blocks = [(2, h) for h in range(HEADS) if h != r] + [(j, r) for j in range(4)]
         PS[r] = (OTH[r] + product(r, 1, blocks)).astype(bf16)
         to_across(r).start()
         OWN[r] = OWN[r] + product(r, 0, blocks)
+
+    for r in range(4):
+        x_pass_on(strided_part(r), 4 + r)
+        if r == 0:
+            for h in range(HEADS):
+                for copy in x_relay(near_part(h), h):
+                    copy.wait_recv()
+        else:
+            finish(r - 1)
+    finish(3)
 
     for r in range(4):
         to_across(r).wait_recv()
@@ -474,7 +499,9 @@
     for d in (1, 2, 3):
         for yr in range(2):
             w_copy(d, yr).wait_send()
-            w_forward(d, yr).wait_send()
+            w_cross(d, yr).wait_send()
+            w_chip(d, yr).wait_send()
+            w_last(d, yr).wait_send()
         for kind in range(4):
             plane_copy(d, kind).wait_send()
         for kind in range(2):
@@ -510,7 +537,7 @@
 def shards(planes, queries, keys, values, out_weight):
     dma = pltpu.SemaphoreType.DMA
     vmem = pltpu.VMEM
-    anywhere = pl.BlockSpec(memory_space=pl.ANY)
+    anywhere = pl.BlockSpec(memory_space=pltpu.HBM)
     return pl.pallas_call(
         functools.partial(layer_kernel, planes),
         name="layer",
@@ -541,6 +568,7 @@
             vmem((4, 256, 512), f32),
             dma((4, 3)), dma((2,)),
             dma((3, 2)), dma((3, 2)), dma((3, 2)), dma((3, 2)),
+            dma((3, 2)), dma((3, 2)), dma((3, 2)), dma((3, 2)),
             dma((4, 2)), dma((4, 2)),
             dma((3, 4)), dma((3, 4)),
             dma((4,)), dma((4,)),
@@ -549,7 +577,7 @@
             dma((4, 2)), dma((4, 2)),
         ] + [dma((8,))] * 8 + [dma((4,))] * 2,
         compiler_params=pltpu.CompilerParams(
-            collective_id=0, has_side_effects=True, vmem_limit_bytes=58 * 1024 * 1024),
+            collective_id=0, has_side_effects=True, vmem_limit_bytes=52 * 1024 * 1024),
     )(queries, keys, values, out_weight)
 
 

time: 94.3 us -> 89.3 us (0.947)
  Pallas kernels: 91 us -> 88.3 us
  local copies, waits for them, and re-layouts: 2.26 us -> 0.97 us
    pallas_call x1, Pallas kernels: 91 us -> 88.3 us  [shards(): pl.pallas_call(functools.partial(layer_kernel, planes), name='layer', out...]
    unnamed x1, local copies, waits for them, and re-layouts: 2.26 us -> 0.97 us
where the time goes in v3:
time: 89.3 us
  Pallas kernels  88.3 us (99%)
  local copies, waits for them, and re-layouts  0.97 us (1%)
    pallas_call x1, Pallas kernels, shards(): pl.pallas_call(functools.partial(layer_kernel, planes), name='layer', out...  88.3 us

profile of v3, /device:TPU:1, one launch (start us, length us, event | category | flops | bytes accessed | tf_op | source)
XLA Modules:
  0.0 89.3 jit_solution(7155883644562698938)
XLA Ops:
  0.0 88.3 %layer.1 = bf16[1024,512]{1,0:T(8,128)(2,1)S(1)} custom-call(bf16[1024,512]{1,0:T(8,128)(2,1)} %q_hbm.1, bf16[1024,512]{1,0:T(8,128)(2,1)} %k_hbm.1, bf16[1024,512]{1,0:T(8,128)(2,1)} %v_hbm.1, bf16[512,4096]{1,0:T(8,128)(2,1)} %w_hbm.1), custom_call_target="tpu_custom_call" | custom-call | tf_op jit(solution)/shard_map/layer/pallas_call | solution.py:541
  88.3 1.0 %copy.6 = bf16[1024,512]{1,0:T(8,128)(2,1)} copy(bf16[1024,512]{1,0:T(8,128)(2,1)S(1)} %layer.1) | data formatting | bytes 2097152

commit v4 on v3

--- a/solution.py
+++ b/solution.py
@@ -344,7 +344,7 @@
             for copy in x_copy(near_part(h), h):
                 copy.start()
 
-        @pl.when(h == 2)
+        @pl.when(h == 3)
         def _():
             for d in (1, 3, 2):
                 for yr in range(2):
@@ -415,26 +415,6 @@
             w_last(d, yr).start()
 
     for d in (1, 2, 3):
-        for yr in range(2):
-            w_chipped(d, yr).wait_recv()
-            w_lasted(d, yr).wait_recv()
-    for yr in range(2):
-        w_own(yr).wait()
-
-    def weight(yr, j, h):
-        return WG[yr, (x + 4 - j) % 4, h * DH:(h + 1) * DH, :]
-
-    def product(r, yr, blocks):
-        left_side = jnp.concatenate([AG[j, h, (r - h) % 4] for j, h in blocks], axis=1)
-        right_side = jnp.concatenate([weight(yr, j, h) for j, h in blocks], axis=0)
-        return jnp.dot(left_side, right_side, preferred_element_type=f32)
-
-    for r in range(4):
-        blocks = [(j, h) for j in (0, 1, 3) for h in range(HEADS) if h != r]
-        for yr, acc in ((1, OTH), (0, OWN)):
-            acc[r] = product(r, yr, blocks)
-
-    for d in (1, 2, 3):
         for kind in range(2):
             back_arrived(d, kind).wait_recv()
 
@@ -465,6 +445,14 @@
 
         for copy in x_copy(strided_part(s), 4 + s):
             copy.start()
+
+    def weight(yr, j, h):
+        return WG[yr, (x + 4 - j) % 4, h * DH:(h + 1) * DH, :]
+
+    def product(r, yr, blocks):
+        left_side = jnp.concatenate([AG[j, h, (r - h) % 4] for j, h in blocks], axis=1)
+        right_side = jnp.concatenate([weight(yr, j, h) for j, h in blocks], axis=0)
+        return jnp.dot(left_side, right_side, preferred_element_type=f32)
 
     def to_across(r):
         return pltpu.make_async_remote_copy(
@@ -478,6 +466,19 @@
         to_across(r).start()
         OWN[r] = OWN[r] + product(r, 0, blocks)
 
+    def begin(r):
+        blocks = [(j, h) for j in (0, 1, 3) for h in range(HEADS) if h != r]
+        for yr, acc in ((1, OTH), (0, OWN)):
+            acc[r] = product(r, yr, blocks)
+
+    for d in (1, 2, 3):
+        for yr in range(2):
+            w_chipped(d, yr).wait_recv()
+            w_lasted(d, yr).wait_recv()
+    for yr in range(2):
+        w_own(yr).wait()
+
+    begin(0)
     for r in range(4):
         x_pass_on(strided_part(r), 4 + r)
         if r == 0:
@@ -486,6 +487,8 @@
                     copy.wait_recv()
         else:
             finish(r - 1)
+        if r < 3:
+            begin(r + 1)
     finish(3)
 
     for r in range(4):

time: 89.3 us -> 91.9 us (1.029)
  the two profiles are of different devices: /device:TPU:1 before, /device:TPU:32 now
where the time goes in v4:
time: 91.9 us; the launch traced here: 91.8 us
  Pallas kernels  90.9 us (99%)
  local copies, waits for them, and re-layouts  0.97 us (1%)
    pallas_call x1, Pallas kernels, shards(): pl.pallas_call(functools.partial(layer_kernel, planes), name='layer', out...  90.9 us

profile of v4, /device:TPU:32, one launch (start us, length us, event | category | flops | bytes accessed | tf_op | source)
XLA Modules:
  0.0 91.8 jit_solution(1423606251110396282)
XLA Ops:
  0.0 90.9 %layer.1 = bf16[1024,512]{1,0:T(8,128)(2,1)S(1)} custom-call(bf16[1024,512]{1,0:T(8,128)(2,1)} %q_hbm.1, bf16[1024,512]{1,0:T(8,128)(2,1)} %k_hbm.1, bf16[1024,512]{1,0:T(8,128)(2,1)} %v_hbm.1, bf16[512,4096]{1,0:T(8,128)(2,1)} %w_hbm.1), custom_call_target="tpu_custom_call" | custom-call | tf_op jit(solution)/shard_map/layer/pallas_call | solution.py:544
  90.9 1.0 %copy.6 = bf16[1024,512]{1,0:T(8,128)(2,1)} copy(bf16[1024,512]{1,0:T(8,128)(2,1)S(1)} %layer.1) | data formatting | bytes 2097152

commit v5 on v4

--- a/solution.py
+++ b/solution.py
@@ -344,7 +344,7 @@
             for copy in x_copy(near_part(h), h):
                 copy.start()
 
-        @pl.when(h == 3)
+        @pl.when(h == 1)
         def _():
             for d in (1, 3, 2):
                 for yr in range(2):
@@ -446,6 +446,13 @@
         for copy in x_copy(strided_part(s), 4 + s):
             copy.start()
 
+    for d in (1, 2, 3):
+        for yr in range(2):
+            w_chipped(d, yr).wait_recv()
+            w_lasted(d, yr).wait_recv()
+    for yr in range(2):
+        w_own(yr).wait()
+
     def weight(yr, j, h):
         return WG[yr, (x + 4 - j) % 4, h * DH:(h + 1) * DH, :]
 
@@ -453,6 +460,11 @@
         left_side = jnp.concatenate([AG[j, h, (r - h) % 4] for j, h in blocks], axis=1)
         right_side = jnp.concatenate([weight(yr, j, h) for j, h in blocks], axis=0)
         return jnp.dot(left_side, right_side, preferred_element_type=f32)
+
+    for r in range(4):
+        blocks = [(j, h) for j in (0, 1, 3) for h in range(HEADS) if h != r]
+        for yr, acc in ((1, OTH), (0, OWN)):
+            acc[r] = product(r, yr, blocks)
 
     def to_across(r):
         return pltpu.make_async_remote_copy(
@@ -466,19 +478,6 @@
         to_across(r).start()
         OWN[r] = OWN[r] + product(r, 0, blocks)
 
-    def begin(r):
-        blocks = [(j, h) for j in (0, 1, 3) for h in range(HEADS) if h != r]
-        for yr, acc in ((1, OTH), (0, OWN)):
-            acc[r] = product(r, yr, blocks)
-
-    for d in (1, 2, 3):
-        for yr in range(2):
-            w_chipped(d, yr).wait_recv()
-            w_lasted(d, yr).wait_recv()
-    for yr in range(2):
-        w_own(yr).wait()
-
-    begin(0)
     for r in range(4):
         x_pass_on(strided_part(r), 4 + r)
         if r == 0:
@@ -487,8 +486,6 @@
                     copy.wait_recv()
         else:
             finish(r - 1)
-        if r < 3:
-            begin(r + 1)
     finish(3)
 
     for r in range(4):

time: 91.9 us -> 84.3 us (0.917)
  the two profiles are of different devices: /device:TPU:32 before, /device:TPU:1 now
where the time goes in v5:
time: 84.3 us; the launch traced here: 84.2 us
  Pallas kernels  83.2 us (99%)
  local copies, waits for them, and re-layouts  0.97 us (1%)
    pallas_call x1, Pallas kernels, shards(): pl.pallas_call(functools.partial(layer_kernel, planes), name='layer', out...  83.2 us

profile of v5, /device:TPU:1, one launch (start us, length us, event | category | flops | bytes accessed | tf_op | source)
XLA Modules:
  0.0 84.2 jit_solution(6224476445329651828)
XLA Ops:
  0.0 83.2 %layer.1 = bf16[1024,512]{1,0:T(8,128)(2,1)S(1)} custom-call(bf16[1024,512]{1,0:T(8,128)(2,1)} %q_hbm.1, bf16[1024,512]{1,0:T(8,128)(2,1)} %k_hbm.1, bf16[1024,512]{1,0:T(8,128)(2,1)} %v_hbm.1, bf16[512,4096]{1,0:T(8,128)(2,1)} %w_hbm.1), custom_call_target="tpu_custom_call" | custom-call | tf_op jit(solution)/shard_map/layer/pallas_call | solution.py:541
  83.2 1.0 %copy.6 = bf16[1024,512]{1,0:T(8,128)(2,1)} copy(bf16[1024,512]{1,0:T(8,128)(2,1)S(1)} %layer.1) | data formatting | bytes 2097152

commit v6 on v4

--- a/solution.py
+++ b/solution.py
@@ -344,7 +344,7 @@
             for copy in x_copy(near_part(h), h):
                 copy.start()
 
-        @pl.when(h == 3)
+        @pl.when(h == 1)
         def _():
             for d in (1, 3, 2):
                 for yr in range(2):

time: 91.9 us -> 84.3 us (0.917)
  the two profiles are of different devices: /device:TPU:32 before, /device:TPU:1 now
where the time goes in v6:
time: 84.3 us; the launch traced here: 84.2 us
  Pallas kernels  83.2 us (99%)
  local copies, waits for them, and re-layouts  0.97 us (1%)
    pallas_call x1, Pallas kernels, shards(): pl.pallas_call(functools.partial(layer_kernel, planes), name='layer', out...  83.2 us

profile of v6, /device:TPU:1, one launch (start us, length us, event | category | flops | bytes accessed | tf_op | source)
XLA Modules:
  0.0 84.2 jit_solution(3576005845569905920)
XLA Ops:
  0.0 83.2 %layer.1 = bf16[1024,512]{1,0:T(8,128)(2,1)S(1)} custom-call(bf16[1024,512]{1,0:T(8,128)(2,1)} %q_hbm.1, bf16[1024,512]{1,0:T(8,128)(2,1)} %k_hbm.1, bf16[1024,512]{1,0:T(8,128)(2,1)} %v_hbm.1, bf16[512,4096]{1,0:T(8,128)(2,1)} %w_hbm.1), custom_call_target="tpu_custom_call" | custom-call | tf_op jit(solution)/shard_map/layer/pallas_call | solution.py:544
  83.2 1.0 %copy.6 = bf16[1024,512]{1,0:T(8,128)(2,1)} copy(bf16[1024,512]{1,0:T(8,128)(2,1)S(1)} %layer.1) | data formatting | bytes 2097152
